TPU v7x, 32 devices: a whole 2x2x4 slice. The times are simulated.
32 devices in a mesh: dp: 8 (over y, x, core), tp: 4 (over z).
Axes of the slice: x: 2, y: 2, z: 4, core: 2. Of those that a mesh axis runs over, the one named last changes fastest.
Arguments:
- feats: bfloat16 [16, 256, 1024], P('dp', 'tp'), may hold values from -12 to 12
- noise: bfloat16 [16, 256, 1024], P('dp', 'tp'), may hold values from -0.59765625 to 0.59765625
- starts: int32 [16, 4], P('dp'), may hold values from 0 to 255
- span_length: int32 [16], P('dp'), may hold values from 1 to 25, as said below
- cotangent: bfloat16 [16, 256, 1024], P('dp', 'tp'), may hold values from -6 to 6
- norm_gains: float32 [5, 1024], replicated, may hold values from 0.1 to 1.9
- ffn1_in: bfloat16 [1024, 4096], P('dp', 'tp'), may hold values from -0.1875 to 0.1875
- ffn1_out: bfloat16 [1024, 4096], P('dp', 'tp'), may hold values from -0.09375 to 0.09375
- qkv_weight: bfloat16 [1024, 3, 1024], P('dp', None, 'tp'), may hold values from -0.1875 to 0.1875
- attn_out: bfloat16 [1024, 1024], P('dp', 'tp'), may hold values from -1.5 to 1.5
- conv_in: bfloat16 [1024, 2, 1024], P('dp', None, 'tp'), may hold values from -0.1875 to 0.1875
- conv_kernel: float32 [5, 1024], replicated, may hold values from -2.5 to 2.5
- batch_gain: float32 [1024], P('tp'), may hold values from 0.1 to 1.9
- batch_bias: float32 [1024], P('tp'), may hold values from -3 to 3
- conv_out: bfloat16 [1024, 1024], P('dp', 'tp'), may hold values from -0.1875 to 0.1875
- ffn2_in: bfloat16 [1024, 4096], P('dp', 'tp'), may hold values from -0.1875 to 0.1875
- ffn2_out: bfloat16 [1024, 4096], P('dp', 'tp'), may hold values from -0.09375 to 0.09375
Outputs:
- layer_out: float32 [16, 256, 1024], P('dp', 'tp')
- feats_grad: float32 [16, 256, 1024], P('dp', 'tp')
- masked_count: float32 [], replicated
- norm_gains_grad: float32 [5, 1024], replicated
- ffn1_in_grad: float32 [1024, 4096], P('dp', 'tp')
- ffn1_out_grad: float32 [1024, 4096], P('dp', 'tp')
- qkv_grad: float32 [1024, 3, 1024], P('dp', None, 'tp')
- attn_out_grad: float32 [1024, 1024], P('dp', 'tp')
- conv_in_grad: float32 [1024, 2, 1024], P('dp', None, 'tp')
- kernel_grad: float32 [5, 1024], replicated
- batch_gain_grad: float32 [1024], P('tp')
- batch_bias_grad: float32 [1024], P('tp')
- conv_out_grad: float32 [1024, 1024], P('dp', 'tp')
- ffn2_in_grad: float32 [1024, 4096], P('dp', 'tp')
- ffn2_out_grad: float32 [1024, 4096], P('dp', 'tp')
Inputs may be any that keep to these rules, and one draw needn't show every extreme that they name: `span_length`: one item has span length 25.
All inputs are finite; a program needn't handle non-finite values.
Results may differ from a plain program's by a relative error of at most 0.02.
Values may be sent and summed in bfloat16 or wider, within the bound.
No kernel may reach another device: no remote copies, remote signals or barrier semaphores. Data moves between devices by JAX's collectives and lax.ppermute only.
A program may use at most 128 MiB of HBM per device.

v0:
```python
import jax
import jax.numpy as jnp
from jax import lax
from jax.sharding import PartitionSpec as P

HEAD_DIM = 128


eps_norm = 1e-05
eps_batch = 1e-05


def span_mask(starts, span_length, anchor, length):
    frames = anchor + jnp.arange(length, dtype=jnp.int32)
    finish = starts + span_length[:, None]
    inside = (frames[None, None, :] >= starts[:, :, None]) & (
        frames[None, None, :] < finish[:, :, None]
    )
    return jnp.any(inside, axis=1)


def normalize(stream, norm_gain):
    centred = stream - jnp.mean(stream, axis=-1, keepdims=True)
    inverse = lax.rsqrt(jnp.mean(centred * centred, axis=-1, keepdims=True) + eps_norm)
    scaled = centred * inverse
    return (scaled * norm_gain, scaled, inverse)


def normalize_back(grad_normed, scaled, inverse, norm_gain):
    grad_scaled = grad_normed * norm_gain
    grad_gain = jnp.sum(grad_normed * scaled, axis=(0, 1))
    centre_term = jnp.mean(grad_scaled, axis=-1, keepdims=True)
    slope_term = jnp.mean(grad_scaled * scaled, axis=-1, keepdims=True)
    return (inverse * (grad_scaled - centre_term - scaled * slope_term), grad_gain)


def swish_slope(values):
    logistic = jax.nn.sigmoid(values)
    return logistic + values * logistic * (1.0 - logistic)


def fetch(weight_in, weight_out):
    return (
        lax.all_gather(weight_in, "dp", axis=0, tiled=True),
        lax.all_gather(weight_out, "dp", axis=0, tiled=True),
    )


def fetch_again(weight_in, weight_out):
    return (
        lax.all_gather(weight_in, "dp", axis=0, tiled=True),
        lax.all_gather(weight_out, "dp", axis=0, tiled=True),
    )


def spread_frames(normed):
    return lax.all_gather(normed.astype(jnp.bfloat16), "tp", axis=1, tiled=True)


def settle_rows(partial_value):
    return lax.psum_scatter(partial_value, "tp", scatter_dimension=1, tiled=True)


def spread_grads(grad_output):
    return lax.all_gather(grad_output.astype(jnp.bfloat16), "tp", axis=1, tiled=True)


def settle_grads(partial_value):
    return lax.psum_scatter(
        partial_value.astype(jnp.bfloat16), "tp", scatter_dimension=1, tiled=True
    ).astype(jnp.float32)


def settle_weights(grad_first, grad_second):
    return (
        lax.psum_scatter(grad_first, "dp", scatter_dimension=0, tiled=True),
        lax.psum_scatter(grad_second, "dp", scatter_dimension=0, tiled=True),
    )


def ffn_forward(stream, norm_gain, weight_in, weight_out):
    normed, scaled, inverse = normalize(stream, norm_gain)
    whole_in = spread_frames(normed)
    hidden = jnp.einsum("itd,df->itf", whole_in, weight_in, preferred_element_type=jnp.float32)
    active = (hidden * jax.nn.sigmoid(hidden)).astype(jnp.bfloat16)
    partial_value = jnp.einsum(
        "itf,df->itd", active, weight_out, preferred_element_type=jnp.float32
    )
    return (stream + 0.5 * settle_rows(partial_value), (scaled, inverse, whole_in, hidden, active))


def ffn_backward(grad_stream, saved, norm_gain, weight_in, weight_out):
    scaled, inverse, whole_in, hidden, active = saved
    whole_grad = spread_grads(0.5 * grad_stream)
    grad_second = jnp.einsum("itd,itf->df", whole_grad, active, preferred_element_type=jnp.float32)
    grad_active = jnp.einsum(
        "itd,df->itf", whole_grad, weight_out, preferred_element_type=jnp.float32
    )
    grad_hidden = (grad_active * swish_slope(hidden)).astype(jnp.bfloat16)
    grad_first = jnp.einsum(
        "itd,itf->df", whole_in, grad_hidden, preferred_element_type=jnp.float32
    )
    grad_normed = settle_grads(
        jnp.einsum("itf,df->itd", grad_hidden, weight_in, preferred_element_type=jnp.float32)
    )
    grad_local, grad_gain = normalize_back(grad_normed, scaled, inverse, norm_gain)
    return (grad_stream + grad_local, grad_gain, grad_first, grad_second)


def split_heads(project):
    items, frames, width = (project.shape[0], project.shape[1], project.shape[3])
    split = project.reshape(items, frames, 3, width // HEAD_DIM, HEAD_DIM)
    return (split[:, :, 0], split[:, :, 1], split[:, :, 2])


def attn_forward(stream, norm_gain, weight_in, weight_out):
    normed, scaled, inverse = normalize(stream, norm_gain)
    whole_in = spread_frames(normed)
    project = jnp.einsum(
        "itd,dch->itch", whole_in, weight_in, preferred_element_type=jnp.float32
    ).astype(jnp.bfloat16)
    queries, key_rows, value_rows = split_heads(project)
    scores = jnp.einsum(
        "iqhe,ikhe->ihqk", queries, key_rows, preferred_element_type=jnp.float32
    ) * HEAD_DIM ** (-0.5)
    highest = jnp.max(scores, axis=-1, keepdims=True)
    log_total = highest + jnp.log(jnp.sum(jnp.exp(scores - highest), axis=-1, keepdims=True))
    probs = jnp.exp(scores - log_total).astype(jnp.bfloat16)
    mixed = jnp.einsum("ihqk,ikhe->iqhe", probs, value_rows, preferred_element_type=jnp.float32)
    mixed = mixed.reshape(project.shape[0], project.shape[1], project.shape[3]).astype(jnp.bfloat16)
    partial_value = jnp.einsum("ite,de->itd", mixed, weight_out, preferred_element_type=jnp.float32)
    return (
        stream + settle_rows(partial_value),
        (scaled, inverse, whole_in, project, log_total, mixed),
    )


def attn_backward(grad_stream, saved, norm_gain, weight_in, weight_out):
    scaled, inverse, whole_in, project, log_total, mixed = saved
    queries, key_rows, value_rows = split_heads(project)
    whole_grad = spread_grads(grad_stream)
    grad_second = jnp.einsum("itd,ite->de", whole_grad, mixed, preferred_element_type=jnp.float32)
    grad_mixed = jnp.einsum(
        "itd,de->ite", whole_grad, weight_out, preferred_element_type=jnp.float32
    ).astype(jnp.bfloat16)
    grad_mixed = grad_mixed.reshape(queries.shape)
    factor = HEAD_DIM ** (-0.5)
    scores = (
        jnp.einsum("iqhe,ikhe->ihqk", queries, key_rows, preferred_element_type=jnp.float32)
        * factor
    )
    probs = jnp.exp(scores - log_total)
    grad_values = jnp.einsum(
        "ihqk,iqhe->ikhe",
        probs.astype(jnp.bfloat16),
        grad_mixed,
        preferred_element_type=jnp.float32,
    )
    grad_probs = jnp.einsum(
        "iqhe,ikhe->ihqk", grad_mixed, value_rows, preferred_element_type=jnp.float32
    )
    grad_scores = (
        probs * (grad_probs - jnp.sum(probs * grad_probs, axis=-1, keepdims=True))
    ).astype(jnp.bfloat16)
    grad_queries = (
        jnp.einsum("ihqk,ikhe->iqhe", grad_scores, key_rows, preferred_element_type=jnp.float32)
        * factor
    )
    grad_keys = (
        jnp.einsum("ihqk,iqhe->ikhe", grad_scores, queries, preferred_element_type=jnp.float32)
        * factor
    )
    grad_project = (
        jnp.stack((grad_queries, grad_keys, grad_values), axis=2)
        .astype(jnp.bfloat16)
        .reshape(project.shape)
    )
    grad_first = jnp.einsum(
        "itd,itch->dch", whole_in, grad_project, preferred_element_type=jnp.float32
    )
    grad_normed = settle_grads(
        jnp.einsum("itch,dch->itd", grad_project, weight_in, preferred_element_type=jnp.float32)
    )
    grad_local, grad_gain = normalize_back(grad_normed, scaled, inverse, norm_gain)
    return (grad_stream + grad_local, grad_gain, grad_first, grad_second)


def depth_mix(kernel_local, gated):
    taps = kernel_local.shape[0]
    reach = taps // 2
    frames = gated.shape[1]
    padded = jnp.pad(gated, ((0, 0), (reach, reach), (0, 0)))
    return (
        padded,
        sum((kernel_local[offset] * padded[:, offset : offset + frames] for offset in range(taps))),
    )


def conv_forward(
    stream, norm_gain, weight_in, kernel_local, batch_gain, batch_bias, weight_out, masked_total
):
    normed, scaled, inverse = normalize(stream, norm_gain)
    whole_in = spread_frames(normed)
    paired = jnp.einsum("itd,dgc->itgc", whole_in, weight_in, preferred_element_type=jnp.float32)
    gated = paired[:, :, 0] * jax.nn.sigmoid(paired[:, :, 1])
    padded, depthwise = depth_mix(kernel_local, gated)
    first_sum = jnp.sum(depthwise, axis=(0, 1))
    second_sum = jnp.sum(depthwise * depthwise, axis=(0, 1))
    first_sum, second_sum = lax.psum((first_sum, second_sum), "dp")
    population = depthwise.shape[0] * depthwise.shape[1] * lax.axis_size("dp")
    average = first_sum / population
    variance = second_sum / population - average * average
    batch_inverse = lax.rsqrt(variance + eps_batch)
    normal = (depthwise - average) * batch_inverse
    batched = normal * batch_gain + batch_bias
    active = (batched * jax.nn.sigmoid(batched)).astype(jnp.bfloat16)
    partial_value = jnp.einsum(
        "itc,dc->itd", active, weight_out, preferred_element_type=jnp.float32
    )
    saved = (scaled, inverse, whole_in, paired, padded, normal, batch_inverse, batched, active)
    return (stream + settle_rows(partial_value), saved, masked_total)


def conv_backward(grad_stream, saved, norm_gain, weight_in, kernel_local, batch_gain, weight_out):
    scaled, inverse, whole_in, paired, padded, normal, batch_inverse, batched, active = saved
    whole_grad = spread_grads(grad_stream)
    grad_second = jnp.einsum("itd,itc->dc", whole_grad, active, preferred_element_type=jnp.float32)
    grad_active = jnp.einsum(
        "itd,dc->itc", whole_grad, weight_out, preferred_element_type=jnp.float32
    )
    grad_batched = grad_active * swish_slope(batched)
    grad_bias, grad_scale = lax.psum(
        (jnp.sum(grad_batched, axis=(0, 1)), jnp.sum(grad_batched * normal, axis=(0, 1))), "dp"
    )
    population = normal.shape[0] * normal.shape[1] * lax.axis_size("dp")
    grad_normal = grad_batched * batch_gain
    grad_depth = batch_inverse * (
        grad_normal
        - batch_gain * grad_bias / population
        - normal * (batch_gain * grad_scale / population)
    )
    taps = kernel_local.shape[0]
    reach = taps // 2
    frames = normal.shape[1]
    grad_kernel = jnp.stack(
        [
            jnp.sum(grad_depth * padded[:, offset : offset + frames], axis=(0, 1))
            for offset in range(taps)
        ]
    )
    grad_padded = jnp.pad(grad_depth, ((0, 0), (reach, reach), (0, 0)))
    grad_gated = sum(
        (
            kernel_local[offset] * grad_padded[:, 2 * reach - offset : 2 * reach - offset + frames]
            for offset in range(taps)
        )
    )
    values_part = paired[:, :, 0]
    logistic = jax.nn.sigmoid(paired[:, :, 1])
    grad_paired = jnp.stack(
        (grad_gated * logistic, grad_gated * values_part * logistic * (1.0 - logistic)), axis=2
    ).astype(jnp.bfloat16)
    grad_first = jnp.einsum(
        "itd,itgc->dgc", whole_in, grad_paired, preferred_element_type=jnp.float32
    )
    grad_normed = settle_grads(
        jnp.einsum("itgc,dgc->itd", grad_paired, weight_in, preferred_element_type=jnp.float32)
    )
    grad_local, grad_gain = normalize_back(grad_normed, scaled, inverse, norm_gain)
    return (
        grad_stream + grad_local,
        grad_gain,
        grad_first,
        grad_second,
        grad_kernel,
        grad_scale,
        grad_bias,
    )


def on_device(
    feats,
    noise,
    starts,
    span_length,
    cotangent,
    norm_gains,
    ffn1_in,
    ffn1_out,
    qkv_weight,
    attn_out,
    conv_in,
    conv_kernel,
    batch_gain,
    batch_bias,
    conv_out,
    ffn2_in,
    ffn2_out,
):
    local_frames = feats.shape[1]
    whole_frames = local_frames * lax.axis_size("tp")
    channels = batch_gain.shape[0]
    channel_start = lax.axis_index("tp") * channels
    masked = span_mask(starts, span_length, lax.axis_index("tp") * local_frames, local_frames)
    group_mask = span_mask(starts, span_length, 0, whole_frames)
    masked_total = jnp.sum(group_mask.astype(jnp.float32))
    masked_total = lax.psum(masked_total, "dp")
    kernel_local = lax.dynamic_slice_in_dim(conv_kernel, channel_start, channels, 1)
    stream = jnp.where(masked[:, :, None], noise, feats).astype(jnp.float32)
    first_weights = fetch(ffn1_in, ffn1_out)
    stream, first_saved = ffn_forward(stream, norm_gains[0], first_weights[0], first_weights[1])
    attn_weights = fetch(qkv_weight, attn_out)
    stream, attn_saved = attn_forward(stream, norm_gains[1], attn_weights[0], attn_weights[1])
    conv_weights = fetch(conv_in, conv_out)
    stream, conv_saved, masked_total = conv_forward(
        stream,
        norm_gains[2],
        conv_weights[0],
        kernel_local,
        batch_gain,
        batch_bias,
        conv_weights[1],
        masked_total,
    )
    second_weights = fetch(ffn2_in, ffn2_out)
    stream, second_saved = ffn_forward(stream, norm_gains[3], second_weights[0], second_weights[1])
    layer_out, final_scaled, final_inverse = normalize(stream, norm_gains[4])
    population = whole_frames * feats.shape[0] * lax.axis_size("dp")
    mask_float = masked[:, :, None].astype(jnp.float32)
    seed = cotangent.astype(jnp.float32) * mask_float * jnp.sqrt(population / masked_total)
    grad_stream, gain_final = normalize_back(seed, final_scaled, final_inverse, norm_gains[4])
    second_back = fetch_again(ffn2_in, ffn2_out)
    grad_stream, gain_second, second_in_grad, second_out_grad = ffn_backward(
        grad_stream, second_saved, norm_gains[3], second_back[0], second_back[1]
    )
    second_in_grad, second_out_grad = settle_weights(second_in_grad, second_out_grad)
    conv_back = fetch_again(conv_in, conv_out)
    (
        grad_stream,
        gain_conv,
        conv_in_grad,
        conv_out_grad,
        kernel_part,
        batch_gain_grad,
        batch_bias_grad,
    ) = conv_backward(
        grad_stream, conv_saved, norm_gains[2], conv_back[0], kernel_local, batch_gain, conv_back[1]
    )
    conv_in_grad, conv_out_grad = settle_weights(conv_in_grad, conv_out_grad)
    attn_back = fetch_again(qkv_weight, attn_out)
    grad_stream, gain_attn, qkv_grad, attn_out_grad = attn_backward(
        grad_stream, attn_saved, norm_gains[1], attn_back[0], attn_back[1]
    )
    qkv_grad, attn_out_grad = settle_weights(qkv_grad, attn_out_grad)
    first_back = fetch_again(ffn1_in, ffn1_out)
    grad_stream, gain_first, first_in_grad, first_out_grad = ffn_backward(
        grad_stream, first_saved, norm_gains[0], first_back[0], first_back[1]
    )
    first_in_grad, first_out_grad = settle_weights(first_in_grad, first_out_grad)
    gain_grads = jnp.stack((gain_first, gain_attn, gain_conv, gain_second, gain_final))
    kernel_full = lax.dynamic_update_slice_in_dim(
        jnp.zeros(conv_kernel.shape, jnp.float32), kernel_part, channel_start, 1
    )
    gain_grads, kernel_grad = lax.psum((gain_grads, kernel_full), ("dp", "tp"))
    feats_grad = jnp.where(masked[:, :, None], 0.0, grad_stream)
    return (
        layer_out,
        feats_grad,
        masked_total,
        gain_grads,
        first_in_grad,
        first_out_grad,
        qkv_grad,
        attn_out_grad,
        conv_in_grad,
        kernel_grad,
        batch_gain_grad,
        batch_bias_grad,
        conv_out_grad,
        second_in_grad,
        second_out_grad,
    )


def solution(mesh):
    return jax.shard_map(
        on_device,
        mesh=mesh,
        in_specs=(
            P("dp", "tp", None),
            P("dp", "tp", None),
            P("dp", None),
            P("dp"),
            P("dp", "tp", None),
            P(),
            P("dp", "tp"),
            P("dp", "tp"),
            P("dp", None, "tp"),
            P("dp", "tp"),
            P("dp", None, "tp"),
            P(),
            P("tp"),
            P("tp"),
            P("dp", "tp"),
            P("dp", "tp"),
            P("dp", "tp"),
        ),
        out_specs=(
            P("dp", "tp", None),
            P("dp", "tp", None),
            P(),
            P(),
            P("dp", "tp"),
            P("dp", "tp"),
            P("dp", None, "tp"),
            P("dp", "tp"),
            P("dp", None, "tp"),
            P(),
            P("tp"),
            P("tp"),
            P("dp", "tp"),
            P("dp", "tp"),
            P("dp", "tp"),
        ),
        check_vma=False,
    )
```

profile of v0, /device:TPU:0, one launch (start us, length us, event | category | flops | bytes accessed | tf_op | source)
XLA Modules:
  0.0 1181.2 jit_solution(10327617241915770338)
XLA Ops:
  13.7 29.3 %all-gather.15.cloned.1.call-done = bf16[2,256,1024]{2,1,0:T(8,128)(2,1)} async-done(((bf16[2,64,1024]{2,1,0:T(8,128)(2,1)}), bf16[2,256,1024]{2,1,0:T(8,128)(2,1)}) %all-gather.15.cloned.1.call-update) | async-done | bytes 1048592 | tf_op jit(solution)/shard_map/all_gather | solution.py:57
  43.0 29.1 %all-gather.17.cloned.1.call-done = bf16[1024,1024]{1,0:T(8,128)(2,1)} async-done(((bf16[128,1024]{1,0:T(8,128)(2,1)}), bf16[1024,1024]{1,0:T(8,128)(2,1)}) %all-gather.17.cloned.1.call-update) | async-done | bytes 2097168 | tf_op jit(solution)/shard_map/all_gather | solution.py:44
  75.3 26.5 %all-gather.19.cloned.1.call-done = bf16[1024,1024]{1,0:T(8,128)(2,1)} async-done(((bf16[128,1024]{1,0:T(8,128)(2,1)}), bf16[1024,1024]{1,0:T(8,128)(2,1)}) %all-gather.19.cloned.1.call-update) | async-done | bytes 2097168 | tf_op jit(solution)/shard_map/all_gather | solution.py:45
  107.8 42.0 %reduce-scatter.17.cloned.1.call-done = f32[2,64,1024]{2,1,0:T(8,128)} async-done(((f32[2,256,1024]{2,1,0:T(8,128)}), f32[2,64,1024]{2,1,0:T(8,128)}) %reduce-scatter.17.cloned.1.call-update) | async-done | bytes 524304 | tf_op jit(solution)/shard_map/reduce_scatter | solution.py:61
  177.2 30.0 %all-gather.21.cloned.1.call-done = bf16[2,256,1024]{2,1,0:T(8,128)(2,1)} async-done(((bf16[2,64,1024]{2,1,0:T(8,128)(2,1)}), bf16[2,256,1024]{2,1,0:T(8,128)(2,1)}) %all-gather.21.cloned.1.call-update) | async-done | bytes 1048592 | tf_op jit(solution)/shard_map/all_gather | solution.py:57
  214.2 42.3 %reduce-scatter.19.cloned.1.call-done = f32[2,64,1024]{2,1,0:T(8,128)} async-done(((f32[2,256,1024]{2,1,0:T(8,128)}), f32[2,64,1024]{2,1,0:T(8,128)}) %reduce-scatter.19.cloned.1.call-update) | async-done | bytes 524304 | tf_op jit(solution)/shard_map/reduce_scatter | solution.py:61
  281.6 30.2 %all-gather.25.cloned.1.call-done = bf16[2,256,1024]{2,1,0:T(8,128)(2,1)} async-done(((bf16[2,64,1024]{2,1,0:T(8,128)(2,1)}), bf16[2,256,1024]{2,1,0:T(8,128)(2,1)}) %all-gather.25.cloned.1.call-update) | async-done | bytes 1048592 | tf_op jit(solution)/shard_map/all_gather | solution.py:57
  333.9 41.1 %reduce-scatter.21.cloned.1.call-done = f32[2,64,1024]{2,1,0:T(8,128)} async-done(((f32[2,256,1024]{2,1,0:T(8,128)}), f32[2,64,1024]{2,1,0:T(8,128)}) %reduce-scatter.21.cloned.1.call-update) | async-done | bytes 524304 | tf_op jit(solution)/shard_map/reduce_scatter | solution.py:61
  378.3 25.6 %all-gather.31.cloned.1.call-done = bf16[1024,1024]{1,0:T(8,128)(2,1)} async-done(((bf16[128,1024]{1,0:T(8,128)(2,1)}), bf16[1024,1024]{1,0:T(8,128)(2,1)}) %all-gather.31.cloned.1.call-update) | async-done | bytes 2097168 | tf_op jit(solution)/shard_map/all_gather | solution.py:44
  403.9 30.0 %all-gather.29.cloned.1.call-done = bf16[2,256,1024]{2,1,0:T(8,128)(2,1)} async-done(((bf16[2,64,1024]{2,1,0:T(8,128)(2,1)}), bf16[2,256,1024]{2,1,0:T(8,128)(2,1)}) %all-gather.29.cloned.1.call-update) | async-done | bytes 1048592 | tf_op jit(solution)/shard_map/all_gather | solution.py:57
  468.6 43.0 %reduce-scatter.23.cloned.1.call-done = f32[2,64,1024]{2,1,0:T(8,128)} async-done(((f32[2,256,1024]{2,1,0:T(8,128)}), f32[2,64,1024]{2,1,0:T(8,128)}) %reduce-scatter.23.cloned.1.call-update) | async-done | bytes 524304 | tf_op jit(solution)/shard_map/reduce_scatter | solution.py:61
  516.3 27.3 %all-gather.35.cloned.1.call-done = bf16[2,256,1024]{2,1,0:T(8,128)(2,1)} async-done(((bf16[2,64,1024]{2,1,0:T(8,128)(2,1)}), bf16[2,256,1024]{2,1,0:T(8,128)(2,1)}) %all-gather.35.cloned.1.call-update) | async-done | bytes 1048592 | tf_op jit(solution)/shard_map/all_gather | solution.py:65
  551.2 26.8 %reduce-scatter.25.cloned.1.call-done = bf16[2,64,1024]{2,1,0:T(8,128)(2,1)} async-done(((bf16[2,256,1024]{2,1,0:T(8,128)(2,1)}), bf16[2,64,1024]{2,1,0:T(8,128)(2,1)}) %reduce-scatter.25.cloned.1.call-update) | async-done | bytes 262160 | tf_op jit(solution)/shard_map/reduce_scatter | solution.py:69
  581.8 26.6 %all-gather.37.cloned.1.call-done = bf16[2,256,1024]{2,1,0:T(8,128)(2,1)} async-done(((bf16[2,64,1024]{2,1,0:T(8,128)(2,1)}), bf16[2,256,1024]{2,1,0:T(8,128)(2,1)}) %all-gather.37.cloned.1.call-update) | async-done | bytes 1048592 | tf_op jit(solution)/shard_map/all_gather | solution.py:65
  659.3 26.6 %all-gather.39.cloned.1.call-done = bf16[2,256,1024]{2,1,0:T(8,128)(2,1)} async-done(((bf16[2,64,1024]{2,1,0:T(8,128)(2,1)}), bf16[2,256,1024]{2,1,0:T(8,128)(2,1)}) %all-gather.39.cloned.1.call-update) | async-done | bytes 1048592 | tf_op jit(solution)/shard_map/all_gather | solution.py:65
  696.1 26.5 %reduce-scatter.29.cloned.1.call-done = bf16[2,64,1024]{2,1,0:T(8,128)(2,1)} async-done(((bf16[2,256,1024]{2,1,0:T(8,128)(2,1)}), bf16[2,64,1024]{2,1,0:T(8,128)(2,1)}) %reduce-scatter.29.cloned.1.call-update) | async-done | bytes 262160 | tf_op jit(solution)/shard_map/reduce_scatter | solution.py:69
  798.3 27.8 %reduce-scatter.31.cloned.1.call-done = bf16[2,64,1024]{2,1,0:T(8,128)(2,1)} async-done(((bf16[2,256,1024]{2,1,0:T(8,128)(2,1)}), bf16[2,64,1024]{2,1,0:T(8,128)(2,1)}) %reduce-scatter.31.cloned.1.call-update) | async-done | bytes 262160 | tf_op jit(solution)/shard_map/reduce_scatter | solution.py:69
  827.4 39.6 %all-reduce.2 = (f32[5,1024]{1,0:T(8,128)}, f32[5,1024]{1,0:T(8,128)}) all-reduce(f32[5,1024]{1,0:T(8,128)S(1)} %stack.72, f32[5,1024]{1,0:T(8,128)S(1)} %constant_dynamic-update-slice_fusion), channel_id=1, replica_groups=mesh['dp'=8,'tp'=4] {'dp','tp'}, use_global_device_ids=true, to_apply=%region_48.49 | all-reduce | flops 10240 | bytes 81920 | tf_op jit(solution)/shard_map/psum | solution.py:364
  869.0 50.6 %reduce-scatter.47.cloned.1.call-done = f32[128,1024]{1,0:T(8,128)} async-done(((f32[1024,1024]{1,0:T(8,128)}), f32[128,1024]{1,0:T(8,128)}) %reduce-scatter.47.cloned.1.call-update) | async-done | bytes 524304 | tf_op jit(solution)/shard_map/reduce_scatter | solution.py:77
  919.7 55.0 %reduce-scatter.45.cloned.1.call-done = f32[128,1024]{1,0:T(8,128)} async-done(((f32[1024,1024]{1,0:T(8,128)}), f32[128,1024]{1,0:T(8,128)}) %reduce-scatter.45.cloned.1.call-update) | async-done | bytes 524304 | tf_op jit(solution)/shard_map/reduce_scatter | solution.py:76
  974.7 39.6 %reduce-scatter.39.cloned.1.call-done = f32[128,256]{1,0:T(8,128)} async-done(((f32[1024,256]{1,0:T(8,128)}), f32[128,256]{1,0:T(8,128)}) %reduce-scatter.39.cloned.1.call-update) | async-done | bytes 131088 | tf_op jit(solution)/shard_map/reduce_scatter | solution.py:77
  1014.3 50.0 %reduce-scatter.37.cloned.1.call-done = f32[128,3,256]{2,0,1:T(8,128)} async-done(((f32[1024,3,256]{2,0,1:T(8,128)}), f32[128,3,256]{2,0,1:T(8,128)}) %reduce-scatter.37.cloned.1.call-update) | async-done | bytes 393232 | tf_op jit(solution)/shard_map/reduce_scatter | solution.py:76
  1064.3 55.1 %reduce-scatter.35.cloned.1.call-done = f32[128,1024]{1,0:T(8,128)} async-done(((f32[1024,1024]{1,0:T(8,128)}), f32[128,1024]{1,0:T(8,128)}) %reduce-scatter.35.cloned.1.call-update) | async-done | bytes 524304 | tf_op jit(solution)/shard_map/reduce_scatter | solution.py:77
  1119.4 55.0 %reduce-scatter.33.cloned.1.call-done = f32[128,1024]{1,0:T(8,128)} async-done(((f32[1024,1024]{1,0:T(8,128)}), f32[128,1024]{1,0:T(8,128)}) %reduce-scatter.33.cloned.1.call-update) | async-done | bytes 524304 | tf_op jit(solution)/shard_map/reduce_scatter | solution.py:76
  (260 shorter events, 289.7 us)
Async XLA Ops:
  12.9 88.9 %all-gather.19.cloned.1.call-start = ((), (), s32[]{:S(2)}) async-start(), calls=%async_computation.18 | async-start | bytes 2359296 | tf_op jit(solution)/shard_map/all_gather | solution.py:45
  13.7 136.2 %reduce-scatter.17.cloned.1.call-start = ((), (), s32[]{:S(2)}) async-start(), calls=%async_computation.19 | async-start | bytes 2621440 | tf_op jit(solution)/shard_map/reduce_scatter | solution.py:61
  106.1 71.1 %all-gather.23.cloned.1.call-start = ((), (), s32[]{:S(2)}) async-start(), calls=%async_computation.21 | async-start | bytes 1769472 | tf_op jit(solution)/shard_map/all_gather | solution.py:44
  107.8 99.4 %all-gather.21.cloned.1.call-start = ((), (), s32[]{:S(2)}) async-start(), calls=%async_computation.20 | async-start | bytes 1310720 | tf_op jit(solution)/shard_map/all_gather | solution.py:57
  152.1 104.4 %reduce-scatter.19.cloned.1.call-start = ((), (), s32[]{:S(2)}) async-start(), calls=%async_computation.22 | async-start | bytes 2621440 | tf_op jit(solution)/shard_map/reduce_scatter | solution.py:61
  213.4 68.2 %all-gather.27.cloned.1.call-start = ((), (), s32[]{:S(2)}) async-start(), calls=%async_computation.24 | async-start | bytes 1179648 | tf_op jit(solution)/shard_map/all_gather | solution.py:44
  214.1 97.6 %all-gather.25.cloned.1.call-start = ((), (), s32[]{:S(2)}) async-start(), calls=%async_computation.23 | async-start | bytes 1310720 | tf_op jit(solution)/shard_map/all_gather | solution.py:57
  258.8 116.2 %reduce-scatter.21.cloned.1.call-start = ((), (), s32[]{:S(2)}) async-start(), calls=%async_computation.25 | async-start | bytes 2621440 | tf_op jit(solution)/shard_map/reduce_scatter | solution.py:61
  333.1 70.8 %all-gather.31.cloned.1.call-start = ((), (), s32[]{:S(2)}) async-start(), calls=%async_computation.27 | async-start | bytes 2359296 | tf_op jit(solution)/shard_map/all_gather | solution.py:44
  333.8 100.1 %all-gather.29.cloned.1.call-start = ((), (), s32[]{:S(2)}) async-start(), calls=%async_computation.26 | async-start | bytes 1310720 | tf_op jit(solution)/shard_map/all_gather | solution.py:57
  377.3 85.7 %all-gather.33.cloned.1.call-start = ((), (), s32[]{:S(2)}) async-start(), calls=%async_computation.28 | async-start | bytes 2359296 | tf_op jit(solution)/shard_map/all_gather | solution.py:45
  378.0 133.6 %reduce-scatter.23.cloned.1.call-start = ((), (), s32[]{:S(2)}) async-start(), calls=%async_computation.29 | async-start | bytes 2621440 | tf_op jit(solution)/shard_map/reduce_scatter | solution.py:61
  467.8 75.8 %all-gather.35.cloned.1.call-start = ((), (), s32[]{:S(2)}) async-start(), calls=%async_computation.30 | async-start | bytes 1310720 | tf_op jit(solution)/shard_map/all_gather | solution.py:65
  581.8 74.3 %reduce-scatter.27.cloned.1.call-start = ((), (), s32[]{:S(2)}) async-start(), calls=%async_computation.33 | async-start | bytes 1310720 | tf_op jit(solution)/shard_map/reduce_scatter | solution.py:69
  659.2 63.4 %reduce-scatter.29.cloned.1.call-start = ((), (), s32[]{:S(2)}) async-start(), calls=%async_computation.35 | async-start | bytes 1310720 | tf_op jit(solution)/shard_map/reduce_scatter | solution.py:69
  726.0 70.5 %reduce-scatter.41.cloned.1.call-start = ((), (), s32[]{:S(2)}) async-start(), calls=%async_computation.42 | async-start | bytes 2359296 | tf_op jit(solution)/shard_map/reduce_scatter | solution.py:76
  729.5 96.6 %reduce-scatter.31.cloned.1.call-start = ((), (), s32[]{:S(2)}) async-start(), calls=%async_computation.37 | async-start | bytes 1310720 | tf_op jit(solution)/shard_map/reduce_scatter | solution.py:69
  760.1 109.0 %reduce-scatter.43.cloned.1.call-start = ((), (), s32[]{:S(2)}) async-start(), calls=%async_computation.43 | async-start | bytes 1179648 | tf_op jit(solution)/shard_map/reduce_scatter | solution.py:77
  763.2 156.5 %reduce-scatter.47.cloned.1.call-start = ((), (), s32[]{:S(2)}) async-start(), calls=%async_computation.45 | async-start | bytes 4718592 | tf_op jit(solution)/shard_map/reduce_scatter | solution.py:77
  768.2 206.4 %reduce-scatter.45.cloned.1.call-start = ((), (), s32[]{:S(2)}) async-start(), calls=%async_computation.44 | async-start | bytes 4718592 | tf_op jit(solution)/shard_map/reduce_scatter | solution.py:76
  773.1 241.2 %reduce-scatter.39.cloned.1.call-start = ((), (), s32[]{:S(2)}) async-start(), calls=%async_computation.41 | async-start | bytes 1179648 | tf_op jit(solution)/shard_map/reduce_scatter | solution.py:77
  775.8 288.5 %reduce-scatter.37.cloned.1.call-start = ((), (), s32[]{:S(2)}) async-start(), calls=%async_computation.40 | async-start | bytes 3538944 | tf_op jit(solution)/shard_map/reduce_scatter | solution.py:76
  779.9 339.5 %reduce-scatter.35.cloned.1.call-start = ((), (), s32[]{:S(2)}) async-start(), calls=%async_computation.39 | async-start | bytes 4718592 | tf_op jit(solution)/shard_map/reduce_scatter | solution.py:77
  786.1 388.3 %reduce-scatter.33.cloned.1.call-start = ((), (), s32[]{:S(2)}) async-start(), calls=%async_computation.38 | async-start | bytes 4718592 | tf_op jit(solution)/shard_map/reduce_scatter | solution.py:76
  (50 other events, 877.8 us)
Sparse Core Ops, SparseCore 0:
  12.3 30.6 all-gather.14
  44.9 27.1 all-gather.16
  74.0 27.7 all-gather.18
  106.2 43.6 reduce-scatter.16
  179.2 27.9 all-gather.20
  213.5 42.9 reduce-scatter.18
  283.8 27.9 all-gather.24
  333.2 41.7 reduce-scatter.20
  376.9 26.9 all-gather.30
  405.9 27.9 all-gather.28
  435.8 27.1 all-gather.32
  468.0 43.6 reduce-scatter.22
  516.4 27.1 all-gather.34
  551.3 26.6 reduce-scatter.24
  696.0 26.6 reduce-scatter.28
  755.9 40.4 reduce-scatter.40
  798.8 27.2 reduce-scatter.30
  829.7 34.5 reduce-scatter.42
  868.2 51.4 reduce-scatter.46
  923.5 51.1 reduce-scatter.44
  978.3 35.9 reduce-scatter.38
  1018.2 46.0 reduce-scatter.36
  1068.2 51.1 reduce-scatter.34
  1123.2 51.1 reduce-scatter.32
  (6 shorter events, 152.0 us)
where the time goes:
time: 1180 us
  waiting for transfers between devices  943 us (80%)
  blocking collectives  87.7 us (7%)
  matrix products  81.1 us (7%)
  other arithmetic  34.6 us (3%)
  local copies, waits for them, and re-layouts  17.3 us (1%)
  between operations  15.9 us (1%)
    reduce_scatter x4, waiting for transfers between devices, settle_rows(): lax.psum_scatter(partial_value, 'tp', scatter_dimension=1, tiled=True)  168 us
    reduce_scatter x4, waiting for transfers between devices, settle_weights(): lax.psum_scatter(grad_first, 'dp', scatter_dimension=0, tiled=True)  166 us
    reduce_scatter x4, waiting for transfers between devices, settle_weights(): lax.psum_scatter(grad_second, 'dp', scatter_dimension=0, tiled=True)  145 us
    all_gather x4, waiting for transfers between devices, spread_frames(): return lax.all_gather(normed.astype(jnp.bfloat16), 'tp', axis=1, tiled=True)  120 us
    reduce_scatter x4, waiting for transfers between devices, settle_grads(): lax.psum_scatter(partial_value.astype(jnp.bfloat16), 'tp', scatter_dimens...  107 us
    all_gather x4, waiting for transfers between devices, spread_grads(): lax.all_gather(grad_output.astype(jnp.bfloat16), 'tp', axis=1, tiled=True)  104 us
    all_gather x4, waiting for transfers between devices, fetch(): lax.all_gather(weight_in, 'dp', axis=0, tiled=True)  79.7 us
    all_gather x2, waiting for transfers between devices, fetch(): lax.all_gather(weight_out, 'dp', axis=0, tiled=True)  51.1 us
  transfers between devices with their start and end apart: 30, of which 29 were waited for; matrix products, arithmetic and copies ran while one was open for 5% of the time, Pallas kernels for 0%

commit v1 on v0

v1 whole, which is shorter than its diff:
```python
import jax
import jax.numpy as jnp
from jax import lax
from jax.sharding import PartitionSpec as P

HEAD_DIM = 128
eps_norm = 1e-05
eps_batch = 1e-05
bf16 = jnp.bfloat16
f32 = jnp.float32


def mm(left, right, left_dim, right_dim):
    return lax.dot_general(
        left, right, (((left_dim,), (right_dim,)), ((), ())), preferred_element_type=f32
    )


def swap(value, axis, distance):
    pairs = [(index, index ^ distance) for index in range(lax.axis_size(axis))]
    return lax.ppermute(value, axis, pairs)


class Cube:
    def __init__(self, size):
        self.bits = size.bit_length() - 1
        middle = tuple(range(self.bits - 1, 0, -1))
        self.first = middle + (0,)
        self.second = middle[::-1] + (0,)
        self.order = sorted(range(size), key=self.key)

    def key(self, label):
        return sum(((label >> bit) & 1) << place for place, bit in enumerate(self.first))

    def runs(self, entries):
        joined = []
        for source, place in entries:
            if joined and joined[-1][0] == source and joined[-1][2] == place:
                joined[-1][2] = place + 1
            else:
                joined.append([source, place, place + 1])
        return joined

    def rows(self, sources, entries, height):
        parts = [
            lax.slice_in_dim(sources[source], low * height, high * height, axis=0)
            for source, low, high in self.runs(entries)
        ]
        return parts[0] if len(parts) == 1 else jnp.concatenate(parts, axis=0)

    def gather(self, shard, order):
        height = shard.shape[0]
        held, labels = shard, [0]
        for bit in order[:-1]:
            taken = swap(held, "dp", 1 << bit)
            entries = [(label, 0, place) for place, label in enumerate(labels)]
            entries += [(label ^ (1 << bit), 1, place) for place, label in enumerate(labels)]
            entries.sort(key=lambda entry: self.key(entry[0]))
            held = self.rows((held, taken), [entry[1:] for entry in entries], height)
            labels = [entry[0] for entry in entries]
        return held, swap(held, "dp", 1)

    def scatter(self, low, high, order):
        labels = [label for label in self.order if not label & 1]
        height = low.shape[0] // len(labels)
        held = low.astype(f32) + swap(high.astype(bf16), "dp", 1).astype(f32)
        for bit in order[-2::-1]:
            held = held.astype(bf16)
            send = [(0, place) for place, label in enumerate(labels) if label >> bit & 1]
            keep = [(0, place) for place, label in enumerate(labels) if not label >> bit & 1]
            taken = swap(self.rows((held,), send, height), "dp", 1 << bit)
            held = self.rows((held,), keep, height).astype(f32) + taken.astype(f32)
            labels = [label for label in labels if not label >> bit & 1]
        return held


def halves(value):
    middle = value.shape[-1] // 2
    return value[..., :middle], value[..., middle:]


def span_mask(starts, span_length, length):
    frames = jnp.arange(length, dtype=jnp.int32)
    finish = starts + span_length[:, None]
    inside = (frames[None, None, :] >= starts[:, :, None]) & (
        frames[None, None, :] < finish[:, :, None]
    )
    return jnp.any(inside, axis=1)


def normalize(stream, norm_gain):
    centred = stream - jnp.mean(stream, axis=-1, keepdims=True)
    inverse = lax.rsqrt(jnp.mean(centred * centred, axis=-1, keepdims=True) + eps_norm)
    scaled = centred * inverse
    return (scaled * norm_gain, scaled, inverse)


def normalize_back(grad_normed, scaled, inverse, norm_gain):
    grad_scaled = grad_normed * norm_gain
    grad_gain = jnp.sum(grad_normed * scaled, axis=0)
    centre_term = jnp.mean(grad_scaled, axis=-1, keepdims=True)
    slope_term = jnp.mean(grad_scaled * scaled, axis=-1, keepdims=True)
    return (inverse * (grad_scaled - centre_term - scaled * slope_term), grad_gain)


def swish_slope(values):
    logistic = jax.nn.sigmoid(values)
    return logistic + values * logistic * (1.0 - logistic)


def join_pair(partial_value):
    mine = partial_value.astype(bf16)
    return mine.astype(f32) + swap(mine, "tp", 1).astype(f32)


def project_in(normed, weight):
    return sum(mm(part, rows, 1, 0) for part, rows in zip(halves(normed), weight))


def project_out(active, weight):
    return jnp.concatenate([mm(active, rows, 1, 1) for rows in weight], axis=1)


def outer(rows_side, columns_side):
    return [mm(part, columns_side, 0, 0).astype(bf16) for part in halves(rows_side)]


def ffn_forward(stream, norm_gain, groups):
    normed, scaled, inverse = normalize(stream, norm_gain)
    whole_in = normed.astype(bf16)
    saved, partial_value = [], 0.0
    for weight_in, weight_out in groups:
        hidden = project_in(whole_in, weight_in)
        active = (hidden * jax.nn.sigmoid(hidden)).astype(bf16)
        partial_value = partial_value + project_out(active, weight_out)
        saved.append((hidden, active))
    return stream + 0.5 * join_pair(partial_value), (scaled, inverse, whole_in, saved)


def ffn_backward(grad_stream, saved, norm_gain, groups):
    scaled, inverse, whole_in, states = saved
    whole_grad = (0.5 * grad_stream).astype(bf16)
    grads, partial_value = [], 0.0
    for (weight_in, weight_out), (hidden, active) in zip(groups, states):
        grad_active = project_in(whole_grad, weight_out)
        grad_hidden = (grad_active * swish_slope(hidden)).astype(bf16)
        partial_value = partial_value + project_out(grad_hidden, weight_in)
        grads.append((outer(whole_in, grad_hidden), outer(whole_grad, active)))
    grad_normed = join_pair(partial_value)
    grad_local, grad_gain = normalize_back(grad_normed, scaled, inverse, norm_gain)
    return grad_stream + grad_local, grad_gain, grads


def split_heads(project):
    quarter = project.shape[1] // 2
    width = quarter // 3
    pieces = []
    for kind in range(3):
        columns = [
            base + kind * width + head
            for base in (0, quarter)
            for head in range(0, width, HEAD_DIM)
        ]
        pieces.append(jnp.stack([project[:, at : at + HEAD_DIM] for at in columns]))
    return pieces


def merge_heads(pieces):
    heads = pieces[0].shape[0] // 2
    return jnp.concatenate(
        [
            piece[base + head]
            for base in (0, heads)
            for piece in pieces
            for head in range(heads)
        ],
        axis=1,
    )


def attn_forward(stream, norm_gain, weight_in, weight_out):
    normed, scaled, inverse = normalize(stream, norm_gain)
    whole_in = normed.astype(bf16)
    project = project_in(whole_in, weight_in).astype(bf16)
    queries, key_rows, value_rows = split_heads(project)
    scores = jnp.einsum(
        "hqe,hke->hqk", queries, key_rows, preferred_element_type=f32
    ) * HEAD_DIM ** (-0.5)
    highest = jnp.max(scores, axis=-1, keepdims=True)
    raised = jnp.exp(scores - highest)
    probs = raised / jnp.sum(raised, axis=-1, keepdims=True)
    mixed = jnp.einsum(
        "hqk,hke->hqe", probs.astype(bf16), value_rows, preferred_element_type=f32
    ).astype(bf16)
    mixed = jnp.concatenate([mixed[head] for head in range(mixed.shape[0])], axis=1)
    partial_value = project_out(mixed, weight_out)
    saved = (scaled, inverse, whole_in, queries, key_rows, value_rows, probs, mixed)
    return stream + join_pair(partial_value), saved


def attn_backward(grad_stream, saved, norm_gain, weight_in, weight_out):
    scaled, inverse, whole_in, queries, key_rows, value_rows, probs, mixed = saved
    whole_grad = grad_stream.astype(bf16)
    grad_second = outer(whole_grad, mixed)
    grad_mixed = project_in(whole_grad, weight_out).astype(bf16)
    heads = queries.shape[0]
    grad_mixed = jnp.stack(
        [grad_mixed[:, head * HEAD_DIM : (head + 1) * HEAD_DIM] for head in range(heads)]
    )
    factor = HEAD_DIM ** (-0.5)
    grad_values = jnp.einsum(
        "hqk,hqe->hke", probs.astype(bf16), grad_mixed, preferred_element_type=f32
    )
    grad_probs = jnp.einsum("hqe,hke->hqk", grad_mixed, value_rows, preferred_element_type=f32)
    grad_scores = (
        probs * (grad_probs - jnp.sum(probs * grad_probs, axis=-1, keepdims=True))
    ).astype(bf16)
    grad_queries = (
        jnp.einsum("hqk,hke->hqe", grad_scores, key_rows, preferred_element_type=f32) * factor
    )
    grad_keys = (
        jnp.einsum("hqk,hqe->hke", grad_scores, queries, preferred_element_type=f32) * factor
    )
    grad_project = merge_heads(
        [part.astype(bf16) for part in (grad_queries, grad_keys, grad_values)]
    )
    grad_first = outer(whole_in, grad_project)
    grad_normed = join_pair(project_out(grad_project, weight_in))
    grad_local, grad_gain = normalize_back(grad_normed, scaled, inverse, norm_gain)
    return grad_stream + grad_local, grad_gain, grad_first, grad_second


def sum_items(rows):
    for bit in range(lax.axis_size("dp").bit_length() - 1):
        rows = rows + swap(rows, "dp", 1 << bit)
    other = swap(rows, "tp", 2)
    first, second = halves(other)
    return rows + jnp.concatenate([second, first], axis=-1)


def shifted(value, amount):
    frames = value.shape[0]
    if amount == 0:
        return value
    edge = jnp.zeros((abs(amount), value.shape[1]), value.dtype)
    if amount > 0:
        return jnp.concatenate([value[amount:], edge], axis=0)
    return jnp.concatenate([edge, value[: frames + amount]], axis=0)


def value_gate(paired):
    quarter = paired.shape[1] // 2
    width = quarter // 2
    return [
        jnp.concatenate(
            [paired[:, at : at + width] for at in (kind * width, quarter + kind * width)], axis=1
        )
        for kind in (0, 1)
    ]


def conv_forward(
    stream, norm_gain, weight_in, kernel_local, batch_gain, batch_bias, weight_out, masked_own, population
):
    normed, scaled, inverse = normalize(stream, norm_gain)
    whole_in = normed.astype(bf16)
    paired = project_in(whole_in, weight_in)
    values_part, gate = value_gate(paired)
    gated = values_part * jax.nn.sigmoid(gate)
    taps = kernel_local.shape[0]
    reach = taps // 2
    depthwise = sum(
        kernel_local[offset] * shifted(gated, offset - reach) for offset in range(taps)
    )
    sums = jnp.stack(
        [
            jnp.sum(depthwise, axis=0),
            jnp.sum(depthwise * depthwise, axis=0),
            jnp.broadcast_to(masked_own, depthwise.shape[1:]),
        ]
    )
    sums = sum_items(sums)
    average = sums[0] / population
    variance = sums[1] / population - average * average
    batch_inverse = lax.rsqrt(variance + eps_batch)
    normal = (depthwise - average) * batch_inverse
    batched = normal * batch_gain + batch_bias
    active = (batched * jax.nn.sigmoid(batched)).astype(bf16)
    partial_value = project_out(active, weight_out)
    saved = (
        scaled, inverse, whole_in, values_part, gate, gated, normal, batch_inverse, batched, active
    )
    return stream + join_pair(partial_value), saved, sums[2, 0]


def conv_backward(
    grad_stream, saved, norm_gain, weight_in, kernel_local, batch_gain, weight_out, population
):
    scaled, inverse, whole_in, values_part, gate, gated, normal, batch_inverse, batched, active = saved
    whole_grad = grad_stream.astype(bf16)
    grad_active = project_in(whole_grad, weight_out)
    grad_batched = grad_active * swish_slope(batched)
    grad_bias, grad_scale = sum_items(
        jnp.stack([jnp.sum(grad_batched, axis=0), jnp.sum(grad_batched * normal, axis=0)])
    )
    grad_second = outer(whole_grad, active)
    grad_depth = (
        batch_inverse
        * batch_gain
        * (grad_batched - grad_bias / population - normal * (grad_scale / population))
    )
    taps = kernel_local.shape[0]
    reach = taps // 2
    grad_kernel = jnp.stack(
        [jnp.sum(grad_depth * shifted(gated, offset - reach), axis=0) for offset in range(taps)]
    )
    grad_gated = sum(
        kernel_local[offset] * shifted(grad_depth, reach - offset) for offset in range(taps)
    )
    logistic = jax.nn.sigmoid(gate)
    first, second = halves((grad_gated * logistic).astype(bf16))
    third, fourth = halves((grad_gated * values_part * logistic * (1.0 - logistic)).astype(bf16))
    grad_paired = jnp.concatenate([first, third, second, fourth], axis=1)
    grad_first = outer(whole_in, grad_paired)
    grad_normed = join_pair(project_out(grad_paired, weight_in))
    grad_local, grad_gain = normalize_back(grad_normed, scaled, inverse, norm_gain)
    return (
        grad_stream + grad_local,
        grad_gain,
        grad_first,
        grad_second,
        grad_kernel,
        grad_scale,
        grad_bias,
    )


def pick(value, index):
    return lax.dynamic_index_in_dim(value, index, 0, keepdims=False)


def on_device(
    feats,
    noise,
    starts,
    span_length,
    cotangent,
    norm_gains,
    ffn1_in,
    ffn1_out,
    qkv_weight,
    attn_out,
    conv_in,
    conv_kernel,
    batch_gain,
    batch_bias,
    conv_out,
    ffn2_in,
    ffn2_out,
):
    local_frames, width = feats.shape[1], feats.shape[2]
    parts = lax.axis_size("tp")
    replicas = lax.axis_size("dp")
    assert parts == 4 and feats.shape[0] == 2
    whole_frames = local_frames * parts
    population = whole_frames * feats.shape[0] * replicas
    place = lax.axis_index("tp")
    item = place // 2
    channels = batch_gain.shape[0]
    cube = Cube(replicas)
    block = width // replicas

    columns = jnp.arange(width, dtype=jnp.int32)
    position = sum(
        jnp.where(columns // block == at, label, 0) for at, label in enumerate(cube.order)
    )
    source = (position ^ lax.axis_index("dp")) * block + columns % block
    moved = columns[:, None] == source[None, :]

    def to_stream(rows):
        return mm(rows, moved.astype(rows.dtype), 1, 0)

    def exact(rows, contract):
        return lax.dot_general(
            rows,
            moved.astype(f32),
            (((1,), (contract,)), ((), ())),
            precision=lax.Precision.HIGHEST,
        )

    masked = span_mask(starts, span_length, whole_frames)
    local_mask = lax.dynamic_slice_in_dim(masked, place * local_frames, local_frames, 1)[:, :, None]
    entered = jnp.stack(
        [jnp.where(local_mask, noise, feats), jnp.where(local_mask, cotangent, jnp.zeros((), bf16))],
        axis=1,
    )

    first_shard = jnp.concatenate([ffn1_in, ffn1_out], axis=1)
    first_other = swap(first_shard, "tp", 2)
    own = pick(entered, item)
    near = jnp.stack([own, swap(pick(entered, 1 - item), "tp", 2)])
    far = swap(near, "tp", 1)
    relative = jnp.stack([near[0], far[0], near[1], far[1]])
    ordered = jnp.stack([pick(relative, place ^ chunk) for chunk in range(parts)])
    ordered = ordered.transpose(1, 0, 2, 3).reshape(2 * whole_frames, width)
    ordered = to_stream(ordered)
    stream, seed = ordered[:whole_frames], ordered[whole_frames:]
    gains = exact(norm_gains, 0)

    hidden_width = ffn1_in.shape[1]
    first_groups = [
        (cube.gather(ffn1_in, cube.first), cube.gather(ffn1_out, cube.second)),
        (
            cube.gather(first_other[:, :hidden_width], cube.first),
            cube.gather(first_other[:, hidden_width:], cube.second),
        ),
    ]
    rows = ffn1_in.shape[0]
    rest = [
        qkv_weight.reshape(rows, -1), attn_out, conv_in.reshape(rows, -1), conv_out, ffn2_in, ffn2_out
    ]
    joined = swap(jnp.concatenate(rest, axis=1), "tp", 2)
    doubled, at = [], 0
    for shard in rest:
        doubled.append(
            jnp.concatenate([shard, joined[:, at : at + shard.shape[1]]], axis=1)
        )
        at += shard.shape[1]
    attn_weights = cube.gather(doubled[0], cube.first), cube.gather(doubled[1], cube.second)
    conv_weights = cube.gather(doubled[2], cube.second), cube.gather(doubled[3], cube.first)
    second_groups = [(cube.gather(doubled[4], cube.first), cube.gather(doubled[5], cube.second))]

    batch_pair = jnp.stack([batch_gain, batch_bias])
    batch_gain, batch_bias = jnp.concatenate([batch_pair, swap(batch_pair, "tp", 2)], axis=1)
    kernel_local = jnp.concatenate(
        [
            lax.dynamic_slice_in_dim(conv_kernel, start * channels, channels, 1)
            for start in (place, place ^ 2)
        ],
        axis=1,
    )

    stream, first_saved = ffn_forward(stream, gains[0], first_groups)
    stream, attn_saved = attn_forward(stream, gains[1], *attn_weights)
    masked_own = jnp.sum(pick(masked, item).astype(f32))
    stream, conv_saved, masked_total = conv_forward(
        stream,
        gains[2],
        conv_weights[0],
        kernel_local,
        batch_gain,
        batch_bias,
        conv_weights[1],
        masked_own,
        population,
    )
    stream, second_saved = ffn_forward(stream, gains[3], second_groups)
    final_out, final_scaled, final_inverse = normalize(stream, gains[4])

    def deliver(value):
        chunks = value.astype(bf16).reshape(parts, local_frames, width)
        both = jnp.concatenate([pick(chunks, place), pick(chunks, place ^ 2)], axis=0)
        both = mm(both, moved.astype(bf16), 1, 1)
        mine = both[:local_frames]
        other = swap(both[local_frames:].astype(bf16), "tp", 2).astype(f32)
        return jnp.stack(
            [jnp.where(item == 0, mine, other), jnp.where(item == 0, other, mine)]
        )

    layer_out = deliver(final_out)
    grad_stream, gain_final = normalize_back(
        seed * jnp.sqrt(population / masked_total), final_scaled, final_inverse, gains[4]
    )

    def settle(low_high, order):
        return cube.scatter(*low_high, order)

    def settle_pair(held):
        mine, other = halves(held)
        return mine + swap(other.astype(bf16), "tp", 2).astype(f32)

    grad_stream, gain_second, second_grads = ffn_backward(
        grad_stream, second_saved, gains[3], second_groups
    )
    second_in_grad = settle_pair(settle(second_grads[0][0], cube.first))
    second_out_grad = settle_pair(settle(second_grads[0][1], cube.second))
    grad_stream, gain_conv, grad_first, grad_second, kernel_part, grad_scale, grad_bias = conv_backward(
        grad_stream,
        conv_saved,
        gains[2],
        conv_weights[0],
        kernel_local,
        batch_gain,
        conv_weights[1],
        population,
    )
    conv_in_grad = settle_pair(settle(grad_first, cube.second)).reshape(conv_in.shape)
    conv_out_grad = settle_pair(settle(grad_second, cube.first))
    grad_stream, gain_attn, grad_first, grad_second = attn_backward(
        grad_stream, attn_saved, gains[1], *attn_weights
    )
    qkv_grad = settle_pair(settle(grad_first, cube.first)).reshape(qkv_weight.shape)
    attn_out_grad = settle_pair(settle(grad_second, cube.second))
    grad_stream, gain_first, first_grads = ffn_backward(
        grad_stream, first_saved, gains[0], first_groups
    )
    other_in = settle(first_grads[1][0], cube.first)
    other_out = settle(first_grads[1][1], cube.second)
    other = swap(jnp.concatenate([other_in, other_out], axis=1).astype(bf16), "tp", 2).astype(f32)
    first_in_grad = settle(first_grads[0][0], cube.first) + other[:, :hidden_width]
    first_out_grad = settle(first_grads[0][1], cube.second) + other[:, hidden_width:]

    gain_grads = jnp.stack((gain_first, gain_attn, gain_conv, gain_second, gain_final))
    gain_grads = 0.5 * exact(gain_grads, 1)
    kernel_full = jnp.zeros(conv_kernel.shape, f32)
    for quarter, start in enumerate((place, place ^ 2)):
        kernel_full = lax.dynamic_update_slice_in_dim(
            kernel_full,
            kernel_part[:, quarter * channels : (quarter + 1) * channels],
            start * channels,
            1,
        )
    small = jnp.concatenate([gain_grads, kernel_full], axis=0)
    for bit in range(cube.bits):
        small = small + swap(small, "dp", 1 << bit)
    small = small + swap(small, "tp", 2)
    small = small + swap(small, "tp", 1)
    norms = norm_gains.shape[0]
    mask_own = pick(masked, item)[:, None]
    feats_grad = deliver(jnp.where(mask_own, 0.0, grad_stream))
    return (
        layer_out,
        feats_grad,
        masked_total,
        small[:norms],
        first_in_grad,
        first_out_grad,
        qkv_grad,
        attn_out_grad,
        conv_in_grad,
        small[norms:],
        grad_scale[:channels],
        grad_bias[:channels],
        conv_out_grad,
        second_in_grad,
        second_out_grad,
    )


def solution(mesh):
    return jax.shard_map(
        on_device,
        mesh=mesh,
        in_specs=(
            P("dp", "tp", None),
            P("dp", "tp", None),
            P("dp", None),
            P("dp"),
            P("dp", "tp", None),
            P(),
            P("dp", "tp"),
            P("dp", "tp"),
            P("dp", None, "tp"),
            P("dp", "tp"),
            P("dp", None, "tp"),
            P(),
            P("tp"),
            P("tp"),
            P("dp", "tp"),
            P("dp", "tp"),
            P("dp", "tp"),
        ),
        out_specs=(
            P("dp", "tp", None),
            P("dp", "tp", None),
            P(),
            P(),
            P("dp", "tp"),
            P("dp", "tp"),
            P("dp", None, "tp"),
            P("dp", "tp"),
            P("dp", None, "tp"),
            P(),
            P("tp"),
            P("tp"),
            P("dp", "tp"),
            P("dp", "tp"),
            P("dp", "tp"),
        ),
        check_vma=False,
    )
```

time: 1180 us -> 585 us (0.50)
  waiting for transfers between devices: 943 us -> 302 us
  blocking collectives: 87.7 us -> 0 us
  starting transfers between devices: 1.64 us -> 88.9 us
  local copies, waits for them, and re-layouts: 17.3 us -> 46.6 us
  other arithmetic: 34.6 us -> 55.3 us
    reduce_scatter x16 -> x0, waiting for transfers between devices: 586 us -> none  [the longest x4 168 us: settle_rows(): lax.psum_scatter(partial_value, 'tp', scatter_dimension=1, tiled=True)]
    all_gather x14 -> x0, waiting for transfers between devices: 354 us -> none  [the longest x4 120 us: spread_frames(): return lax.all_gather(normed.astype(jnp.bfloat16), 'tp', axis=1, tiled=True)]
    ppermute x0 -> x95, waiting for transfers between devices: none -> 302 us  [swap(): return lax.ppermute(value, axis, pairs)]
    ppermute x0 -> x95, starting transfers between devices: none -> 88.9 us  [swap(): return lax.ppermute(value, axis, pairs)]
    psum x3 -> x0, blocking collectives: 66.6 us -> none  [the longest x1 39.6 us: on_device(): gain_grads, kernel_grad = lax.psum((gain_grads, kernel_full), ('dp', 'tp'))]
    all_gather x2 -> x0, blocking collectives: 21.1 us -> none  [fetch(): lax.all_gather(weight_out, 'dp', axis=0, tiled=True)]
    unnamed x91 -> x479, local copies, waits for them, and re-layouts: 13.8 us -> 29.7 us
    concatenate x0 -> x40, other arithmetic: none -> 14.6 us  [the longest x24 10.2 us: rows(): return parts[0] if len(parts) == 1 else jnp.concatenate(parts, axis=0)]
  transfers between devices with their start and end apart: 30 -> 95, of which waited for: 29 -> 43; matrix products, arithmetic and copies ran while one was open for 5% -> 23% of each run, Pallas kernels for 0% -> 0%
where the time goes in v1:
time: 585 us; the launch traced here: 575 us
  waiting for transfers between devices  302 us (52%)
  starting transfers between devices  88.9 us (15%)
  matrix products  76.4 us (13%)
  other arithmetic  55.3 us (9%)
  local copies, waits for them, and re-layouts  46.6 us (8%)
    ppermute x95, waiting for transfers between devices, swap(): return lax.ppermute(value, axis, pairs)  302 us
    ppermute x95, starting transfers between devices, swap(): return lax.ppermute(value, axis, pairs)  88.9 us
    dot_general x63, matrix products, mm(): lax.dot_general(left, right, (((left_dim,), (right_dim,)), ((), ())), pre...  66.8 us
    unnamed x479, local copies, waits for them, and re-layouts  29.7 us
  transfers between devices with their start and end apart: 95, of which 43 were waited for; matrix products, arithmetic and copies ran while one was open for 23% of the time, Pallas kernels for 0%

profile of v1, /device:TPU:0, one launch (start us, length us, event | category | flops | bytes accessed | tf_op | source)
XLA Modules:
  0.0 574.6 jit_solution(17605205453977875439)
XLA Ops:
  25.8 17.4 %collective-permute-done.31 = f32[2,256]{1,0:T(2,128)S(1)} collective-permute-done((f32[2,256]{1,0:T(2,128)S(1)}, f32[2,256]{1,0:T(2,128)S(1)}, u32[]{:S(2)}, u32[]{:S(2)}) %collective-permute-start.31) | collective-permute-done | bytes 2080 | tf_op jit(solution)/shard_map/ppermute | solution.py:21
  46.5 4.1 collective-permute-start.1
  64.0 11.5 %collective-permute-done.1 = bf16[2,2,64,1024]{3,2,0,1:T(8,128)(2,1)S(1)} collective-permute-done((bf16[2,2,64,1024]{3,2,0,1:T(8,128)(2,1)S(1)}, bf16[2,2,64,1024]{3,2,0,1:T(8,128)(2,1)S(1)}, u32[]{:S(2)}, u32[]{:S(2)}) %collective-permute-start.1) | collective-permute-done | bytes 524320 | tf_op jit(solution)/shard_map/ppermute | solution.py:21
  81.4 6.9 %collective-permute-done.16 = bf16[128,3840]{0,1:T(8,128)(2,1)S(1)} collective-permute-done((bf16[128,3840]{0,1:T(8,128)(2,1)}, bf16[128,3840]{0,1:T(8,128)(2,1)S(1)}, u32[]{:S(2)}, u32[]{:S(2)}) %collective-permute-start.16) | collective-permute-done | bytes 983072 | tf_op jit(solution)/shard_map/ppermute | solution.py:21
  98.7 8.2 %collective-permute-done.17 = bf16[128,1536]{0,1:T(8,128)(2,1)S(1)} collective-permute-done((bf16[128,1536]{0,1:T(8,128)(2,1)S(1)}, bf16[128,1536]{0,1:T(8,128)(2,1)S(1)}, u32[]{:S(2)}, u32[]{:S(2)}) %collective-permute-start.17) | collective-permute-done | bytes 393248 | tf_op jit(solution)/shard_map/ppermute | solution.py:21
  118.0 15.0 %collective-permute-done.18 = bf16[256,1536]{0,1:T(8,128)(2,1)S(1)} collective-permute-done((bf16[256,1536]{0,1:T(8,128)(2,1)S(1)}, bf16[256,1536]{0,1:T(8,128)(2,1)S(1)}, u32[]{:S(2)}, u32[]{:S(2)}) %collective-permute-start.18) | collective-permute-done | bytes 786464 | tf_op jit(solution)/shard_map/ppermute | solution.py:21
  134.8 11.2 %collective-permute-done.15 = bf16[256,1024]{1,0:T(8,128)(2,1)S(1)} collective-permute-done((bf16[256,1024]{1,0:T(8,128)(2,1)S(1)}, bf16[256,1024]{1,0:T(8,128)(2,1)S(1)}, u32[]{:S(2)}, u32[]{:S(2)}) %collective-permute-start.15) | collective-permute-done | bytes 524320 | tf_op jit(solution)/shard_map/ppermute | solution.py:21
  160.6 11.0 %collective-permute-done.23 = bf16[256,1024]{1,0:T(8,128)(2,1)S(1)} collective-permute-done((bf16[256,1024]{1,0:T(8,128)(2,1)S(1)}, bf16[256,1024]{1,0:T(8,128)(2,1)S(1)}, u32[]{:S(2)}, u32[]{:S(2)}) %collective-permute-start.23) | collective-permute-done | bytes 524320 | tf_op jit(solution)/shard_map/ppermute | solution.py:21
  179.6 15.9 %collective-permute-done.28 = f32[3,512]{1,0:T(4,128)S(1)} collective-permute-done((f32[3,512]{1,0:T(4,128)S(1)}, f32[3,512]{1,0:T(4,128)S(1)}, u32[]{:S(2)}, u32[]{:S(2)}) %collective-permute-start.28) | collective-permute-done | bytes 6176 | tf_op jit(solution)/shard_map/ppermute | solution.py:21
  208.5 12.0 %collective-permute-done.40 = bf16[256,2048]{0,1:T(8,128)(2,1)S(1)} collective-permute-done((bf16[256,2048]{0,1:T(8,128)(2,1)S(1)}, bf16[256,2048]{0,1:T(8,128)(2,1)S(1)}, u32[]{:S(2)}, u32[]{:S(2)}) %collective-permute-start.40) | collective-permute-done | bytes 1048608 | tf_op jit(solution)/shard_map/ppermute | solution.py:21
  231.3 11.4 %collective-permute-done.42 = bf16[256,1024]{1,0:T(8,128)(2,1)} collective-permute-done((bf16[256,1024]{1,0:T(8,128)(2,1)}, bf16[256,1024]{1,0:T(8,128)(2,1)}, u32[]{:S(2)}, u32[]{:S(2)}) %collective-permute-start.42) | collective-permute-done | bytes 524320 | tf_op jit(solution)/shard_map/ppermute | solution.py:21
  255.6 11.5 %collective-permute-done.44 = bf16[256,1024]{1,0:T(8,128)(2,1)S(1)} collective-permute-done((bf16[256,1024]{1,0:T(8,128)(2,1)S(1)}, bf16[256,1024]{1,0:T(8,128)(2,1)S(1)}, u32[]{:S(2)}, u32[]{:S(2)}) %collective-permute-start.44) | collective-permute-done | bytes 524320 | tf_op jit(solution)/shard_map/ppermute | solution.py:21
  307.0 6.1 %collective-permute-done.49 = bf16[256,1024]{1,0:T(8,128)(2,1)} collective-permute-done((bf16[256,1024]{1,0:T(8,128)(2,1)}, bf16[256,1024]{1,0:T(8,128)(2,1)}, u32[]{:S(2)}, u32[]{:S(2)}) %collective-permute-start.49) | collective-permute-done | bytes 524320 | tf_op jit(solution)/shard_map/ppermute | solution.py:21
  331.7 8.9 %collective-permute-done.86 = bf16[128,256]{1,0:T(8,128)(2,1)S(1)} collective-permute-done((bf16[128,256]{1,0:T(8,128)(2,1)S(1)}, bf16[128,256]{1,0:T(8,128)(2,1)S(1)}, u32[]{:S(2)}, u32[]{:S(2)}) %collective-permute-start.86) | collective-permute-done | bytes 65568 | tf_op jit(solution)/shard_map/ppermute | solution.py:21
  408.4 5.6 collective-permute-done.52
  414.9 4.9 collective-permute-done.56
  425.0 8.8 %collective-permute-done.82 = bf16[128,512]{1,0:T(8,128)(2,1)S(1)} collective-permute-done((bf16[128,512]{1,0:T(8,128)(2,1)S(1)}, bf16[128,512]{1,0:T(8,128)(2,1)S(1)}, u32[]{:S(2)}, u32[]{:S(2)}) %collective-permute-start.82) | collective-permute-done | bytes 131104 | tf_op jit(solution)/shard_map/ppermute | solution.py:21
  450.5 10.6 %collective-permute-done.88 = bf16[256,2048]{1,0:T(8,128)(2,1)S(1)} collective-permute-done((bf16[256,2048]{1,0:T(8,128)(2,1)}, bf16[256,2048]{1,0:T(8,128)(2,1)S(1)}, u32[]{:S(2)}, u32[]{:S(2)}) %collective-permute-start.88) | collective-permute-done | bytes 1048608 | tf_op jit(solution)/shard_map/ppermute | solution.py:21
  466.3 9.0 %collective-permute-done.65 = bf16[256,1024]{1,0:T(8,128)(2,1)S(1)} collective-permute-done((bf16[256,1024]{1,0:T(8,128)(2,1)S(1)}, bf16[256,1024]{1,0:T(8,128)(2,1)S(1)}, u32[]{:S(2)}, u32[]{:S(2)}) %collective-permute-start.65) | collective-permute-done | bytes 524320 | tf_op jit(solution)/shard_map/ppermute | solution.py:21
  478.5 5.0 collective-permute-done.59
  488.1 28.6 %collective-permute-done.66 = bf16[128,1024]{1,0:T(8,128)(2,1)S(1)} collective-permute-done((bf16[128,1024]{1,0:T(8,128)(2,1)S(1)}, bf16[128,1024]{1,0:T(8,128)(2,1)S(1)}, u32[]{:S(2)}, u32[]{:S(2)}) %collective-permute-start.66) | collective-permute-done | bytes 262176 | tf_op jit(solution)/shard_map/ppermute | solution.py:21
  523.0 10.1 %collective-permute-done.73 = bf16[128,1536]{1,0:T(8,128)(2,1)S(1)} collective-permute-done((bf16[128,1536]{1,0:T(8,128)(2,1)S(1)}, bf16[128,1536]{1,0:T(8,128)(2,1)S(1)}, u32[]{:S(2)}, u32[]{:S(2)}) %collective-permute-start.73) | collective-permute-done | bytes 393248 | tf_op jit(solution)/shard_map/ppermute | solution.py:21
  533.2 26.1 %collective-permute-done.90 = bf16[128,1024]{1,0:T(8,128)(2,1)S(1)} collective-permute-done((bf16[128,1024]{1,0:T(8,128)(2,1)S(1)}, bf16[128,1024]{1,0:T(8,128)(2,1)S(1)}, u32[]{:S(2)}, u32[]{:S(2)}) %collective-permute-start.90) | collective-permute-done | bytes 262176 | tf_op jit(solution)/shard_map/ppermute | solution.py:21
  560.2 9.0 %collective-permute-done.94 = bf16[128,1024]{1,0:T(8,128)(2,1)S(1)} collective-permute-done((bf16[128,1024]{1,0:T(8,128)(2,1)S(1)}, bf16[128,1024]{1,0:T(8,128)(2,1)S(1)}, u32[]{:S(2)}, u32[]{:S(2)}) %collective-permute-start.94) | collective-permute-done | bytes 262176 | tf_op jit(solution)/shard_map/ppermute | solution.py:21
  (938 shorter events, 300.4 us)
Async XLA Ops:
  4.4 41.1 %collective-permute-start = (bf16[2,64,1024]{2,1,0:T(8,128)(2,1)}, bf16[2,64,1024]{2,1,0:T(8,128)(2,1)}, u32[]{:S(2)}, u32[]{:S(2)}) collective-permute-start(bf16[2,64,1024]{2,1,0:T(8,128)(2,1)} %get-tuple-element.182), channel_id=1, source_target_pairs={{0,2},{1,3},{2,0},{3,1},{4,6},{5,7},{6,4},{7,5},{8,10},{9,11},{10,... | collective-permute-start | bytes 786440 | tf_op jit(solution)/shard_map/ppermute | solution.py:21
  10.0 43.3 %collective-permute-start.5 = (bf16[128,1024]{1,0:T(8,128)(2,1)S(1)}, bf16[128,1024]{1,0:T(8,128)(2,1)}, u32[]{:S(2)}, u32[]{:S(2)}) collective-permute-start(bf16[128,1024]{1,0:T(8,128)(2,1)S(1)} %copy-done.89), channel_id=1, source_target_pairs={{0,8},{4,12},{8,0},{12,4},{16,24},{20,28},{24,16},{28,20},{1,9},{5... | collective-permute-start | bytes 786440 | tf_op jit(solution)/shard_map/ppermute | solution.py:21
  12.3 38.3 %collective-permute-start.8 = (bf16[128,2048]{1,0:T(8,128)(2,1)}, bf16[128,2048]{1,0:T(8,128)(2,1)}, u32[]{:S(2)}, u32[]{:S(2)}) collective-permute-start(bf16[128,2048]{1,0:T(8,128)(2,1)} %pad_maximum_fusion.16), channel_id=1, source_target_pairs={{0,2},{1,3},{2,0},{3,1},{4,6},{5,7},{6,4},{7,5},{8,10},{9,11},{10,... | collective-permute-start | bytes 1572872 | tf_op jit(solution)/shard_map/ppermute | solution.py:21
  43.2 45.1 %collective-permute-start.16 = (bf16[128,3840]{0,1:T(8,128)(2,1)}, bf16[128,3840]{0,1:T(8,128)(2,1)S(1)}, u32[]{:S(2)}, u32[]{:S(2)}) collective-permute-start(bf16[128,3840]{0,1:T(8,128)(2,1)} %constant_dynamic-update-slice_fusion.3), channel_id=1, source_target_pairs={{0,2},{1,3},{2,0},{3,1},{4,6},{5,7},{6,4},{7,5},{8,10},{9,11},{10,... | collective-permute-start | bytes 2949128 | tf_op jit(solution)/shard_map/ppermute | solution.py:21
  60.4 48.1 %collective-permute-start.4 = (bf16[512,1024]{1,0:T(8,128)(2,1)S(1)}, bf16[512,1024]{1,0:T(8,128)(2,1)S(1)}, u32[]{:S(2)}, u32[]{:S(2)}) collective-permute-start(bf16[512,1024]{1,0:T(8,128)(2,1)S(1)} %constant_dynamic-update-slice_fusion), channel_id=1, source_target_pairs={{0,4},{4,0},{8,12},{12,8},{16,20},{20,16},{24,28},{28,24},{1,5},{5... | collective-permute-start | bytes 3145736 | tf_op jit(solution)/shard_map/ppermute | solution.py:21
  97.1 36.1 %collective-permute-start.24 = (bf16[128,1024]{0,1:T(8,128)(2,1)S(1)}, bf16[128,1024]{0,1:T(8,128)(2,1)S(1)}, u32[]{:S(2)}, u32[]{:S(2)}) collective-permute-start(bf16[128,1024]{0,1:T(8,128)(2,1)S(1)} %pad_maximum_fusion.44), channel_id=1, source_target_pairs={{0,8},{4,12},{8,0},{12,4},{16,24},{20,28},{24,16},{28,20},{1,9},{5... | collective-permute-start | bytes 786440 | tf_op jit(solution)/shard_map/ppermute | solution.py:21
  97.8 59.7 %collective-permute-start.36 = (bf16[128,2048]{0,1:T(8,128)(2,1)}, bf16[128,2048]{0,1:T(8,128)(2,1)}, u32[]{:S(2)}, u32[]{:S(2)}) collective-permute-start(bf16[128,2048]{0,1:T(8,128)(2,1)} %pad_maximum_fusion.25), channel_id=1, source_target_pairs={{0,16},{4,20},{8,24},{12,28},{16,0},{20,4},{24,8},{28,12},{1,17},{... | collective-permute-start | bytes 1572872 | tf_op jit(solution)/shard_map/ppermute | solution.py:21
  115.8 62.7 %collective-permute-start.33 = (bf16[256,512]{0,1:T(8,128)(2,1)}, bf16[256,512]{0,1:T(8,128)(2,1)}, u32[]{:S(2)}, u32[]{:S(2)}) collective-permute-start(bf16[256,512]{0,1:T(8,128)(2,1)} %pad_maximum_fusion.45), channel_id=1, source_target_pairs={{0,8},{4,12},{8,0},{12,4},{16,24},{20,28},{24,16},{28,20},{1,9},{5... | collective-permute-start | bytes 786440 | tf_op jit(solution)/shard_map/ppermute | solution.py:21
  158.6 42.6 %collective-permute-start.37 = (bf16[256,2048]{0,1:T(8,128)(2,1)S(1)}, bf16[256,2048]{0,1:T(8,128)(2,1)S(1)}, u32[]{:S(2)}, u32[]{:S(2)}) collective-permute-start(bf16[256,2048]{0,1:T(8,128)(2,1)S(1)} %pad_maximum_fusion.9), channel_id=1, source_target_pairs={{0,8},{4,12},{8,0},{12,4},{16,24},{20,28},{24,16},{28,20},{1,9},{5... | collective-permute-start | bytes 3145736 | tf_op jit(solution)/shard_map/ppermute | solution.py:21
  285.2 93.7 %collective-permute-start.87 = (bf16[512,2048]{1,0:T(8,128)(2,1)}, bf16[512,2048]{1,0:T(8,128)(2,1)}, u32[]{:S(2)}, u32[]{:S(2)}) collective-permute-start(bf16[512,2048]{1,0:T(8,128)(2,1)} %convolution_convert_fusion.2), channel_id=1, source_target_pairs={{0,4},{4,0},{8,12},{12,8},{16,20},{20,16},{24,28},{28,24},{1,5},{5... | collective-permute-start | bytes 6291464 | tf_op jit(solution)/shard_map/ppermute | solution.py:21
  285.2 97.6 %collective-permute-start.91 = (bf16[512,2048]{1,0:T(8,128)(2,1)}, bf16[512,2048]{1,0:T(8,128)(2,1)}, u32[]{:S(2)}, u32[]{:S(2)}) collective-permute-start(bf16[512,2048]{1,0:T(8,128)(2,1)} %convolution_convert_fusion), channel_id=1, source_target_pairs={{0,4},{4,0},{8,12},{12,8},{16,20},{20,16},{24,28},{28,24},{1,5},{5... | collective-permute-start | bytes 6291464 | tf_op jit(solution)/shard_map/ppermute | solution.py:21
  300.6 58.5 %collective-permute-start.79 = (bf16[512,1024]{1,0:T(8,128)(2,1)}, bf16[512,1024]{1,0:T(8,128)(2,1)}, u32[]{:S(2)}, u32[]{:S(2)}) collective-permute-start(bf16[512,1024]{1,0:T(8,128)(2,1)} %convolution_convert_fusion.6), channel_id=1, source_target_pairs={{0,4},{4,0},{8,12},{12,8},{16,20},{20,16},{24,28},{28,24},{1,5},{5... | collective-permute-start | bytes 3145736 | tf_op jit(solution)/shard_map/ppermute | solution.py:21
  340.6 106.7 %collective-permute-start.71 = (bf16[512,1536]{1,0:T(8,128)(2,1)}, bf16[512,1536]{1,0:T(8,128)(2,1)}, u32[]{:S(2)}, u32[]{:S(2)}) collective-permute-start(bf16[512,1536]{1,0:T(8,128)(2,1)} %convolution_convert_fusion.4), channel_id=1, source_target_pairs={{0,4},{4,0},{8,12},{12,8},{16,20},{20,16},{24,28},{28,24},{1,5},{5... | collective-permute-start | bytes 4718600 | tf_op jit(solution)/shard_map/ppermute | solution.py:21
  378.2 56.6 %collective-permute-start.64 = (bf16[512,1024]{1,0:T(8,128)(2,1)}, bf16[512,1024]{1,0:T(8,128)(2,1)}, u32[]{:S(2)}, u32[]{:S(2)}) collective-permute-start(bf16[512,1024]{1,0:T(8,128)(2,1)} %convolution_convert_fusion.10), channel_id=1, source_target_pairs={{0,4},{4,0},{8,12},{12,8},{16,20},{20,16},{24,28},{28,24},{1,5},{5... | collective-permute-start | bytes 3145736 | tf_op jit(solution)/shard_map/ppermute | solution.py:21
  378.9 58.0 %collective-permute-start.61 = (bf16[512,1024]{1,0:T(8,128)(2,1)}, bf16[512,1024]{1,0:T(8,128)(2,1)}, u32[]{:S(2)}, u32[]{:S(2)}) collective-permute-start(bf16[512,1024]{1,0:T(8,128)(2,1)} %convolution_convert_fusion.12), channel_id=1, source_target_pairs={{0,4},{4,0},{8,12},{12,8},{16,20},{20,16},{24,28},{28,24},{1,5},{5... | collective-permute-start | bytes 3145736 | tf_op jit(solution)/shard_map/ppermute | solution.py:21
  447.3 39.2 %collective-permute-start.69 = (bf16[256,1024]{1,0:T(8,128)(2,1)S(1)}, bf16[256,1024]{1,0:T(8,128)(2,1)S(1)}, u32[]{:S(2)}, u32[]{:S(2)}) collective-permute-start(bf16[256,1024]{1,0:T(8,128)(2,1)S(1)} %pad_maximum_fusion.36), channel_id=1, source_target_pairs={{0,16},{4,20},{8,24},{12,28},{16,0},{20,4},{24,8},{28,12},{1,17},{... | collective-permute-start | bytes 1572872 | tf_op jit(solution)/shard_map/ppermute | solution.py:21
  464.0 54.5 %collective-permute-start.72 = (bf16[256,1536]{1,0:T(8,128)(2,1)S(1)}, bf16[256,1536]{1,0:T(8,128)(2,1)S(1)}, u32[]{:S(2)}, u32[]{:S(2)}) collective-permute-start(bf16[256,1536]{1,0:T(8,128)(2,1)S(1)} %slice.892), channel_id=1, source_target_pairs={{0,8},{4,12},{8,0},{12,4},{16,24},{20,28},{24,16},{28,20},{1,9},{5... | collective-permute-start | bytes 2359304 | tf_op jit(solution)/shard_map/ppermute | solution.py:21
  475.3 43.6 %collective-permute-start.89 = (bf16[128,2048]{1,0:T(8,128)(2,1)S(1)}, bf16[128,2048]{1,0:T(8,128)(2,1)S(1)}, u32[]{:S(2)}, u32[]{:S(2)}) collective-permute-start(bf16[128,2048]{1,0:T(8,128)(2,1)S(1)} %slice.925), channel_id=1, source_target_pairs={{0,16},{4,20},{8,24},{12,28},{16,0},{20,4},{24,8},{28,12},{1,17},{... | collective-permute-start | bytes 1572872 | tf_op jit(solution)/shard_map/ppermute | solution.py:21
  476.8 43.0 %collective-permute-start.93 = (bf16[128,2048]{1,0:T(8,128)(2,1)S(1)}, bf16[128,2048]{1,0:T(8,128)(2,1)S(1)}, u32[]{:S(2)}, u32[]{:S(2)}) collective-permute-start(bf16[128,2048]{1,0:T(8,128)(2,1)S(1)} %slice.933), channel_id=1, source_target_pairs={{0,8},{4,12},{8,0},{12,4},{16,24},{20,28},{24,16},{28,20},{1,9},{5... | collective-permute-start | bytes 1572872 | tf_op jit(solution)/shard_map/ppermute | solution.py:21
  516.7 53.4 %collective-permute-start.70 = (bf16[128,1024]{1,0:T(8,128)(2,1)S(1)}, bf16[128,1024]{1,0:T(8,128)(2,1)S(1)}, u32[]{:S(2)}, u32[]{:S(2)}) collective-permute-start(bf16[128,1024]{1,0:T(8,128)(2,1)S(1)} %slice.889), channel_id=1, source_target_pairs={{0,8},{4,12},{8,0},{12,4},{16,24},{20,28},{24,16},{28,20},{1,9},{5... | collective-permute-start | bytes 786440 | tf_op jit(solution)/shard_map/ppermute | solution.py:21
  517.1 53.1 %collective-permute-start.60 = (bf16[128,1024]{1,0:T(8,128)(2,1)S(1)}, bf16[128,1024]{1,0:T(8,128)(2,1)S(1)}, u32[]{:S(2)}, u32[]{:S(2)}) collective-permute-start(bf16[128,1024]{1,0:T(8,128)(2,1)S(1)} %slice.872), channel_id=1, source_target_pairs={{0,16},{4,20},{8,24},{12,28},{16,0},{20,4},{24,8},{28,12},{1,17},{... | collective-permute-start | bytes 786440 | tf_op jit(solution)/shard_map/ppermute | solution.py:21
  518.5 51.5 %collective-permute-start.67 = (bf16[128,2048]{1,0:T(8,128)(2,1)S(1)}, bf16[128,2048]{1,0:T(8,128)(2,1)S(1)}, u32[]{:S(2)}, u32[]{:S(2)}) collective-permute-start(bf16[128,2048]{1,0:T(8,128)(2,1)S(1)} %pad_maximum_fusion.35), channel_id=1, source_target_pairs={{0,2},{1,3},{2,0},{3,1},{4,6},{5,7},{6,4},{7,5},{8,10},{9,11},{10,... | collective-permute-start | bytes 1572872 | tf_op jit(solution)/shard_map/ppermute | solution.py:21
  519.9 39.5 %collective-permute-start.90 = (bf16[128,1024]{1,0:T(8,128)(2,1)S(1)}, bf16[128,1024]{1,0:T(8,128)(2,1)S(1)}, u32[]{:S(2)}, u32[]{:S(2)}) collective-permute-start(bf16[128,1024]{1,0:T(8,128)(2,1)S(1)} %slice.1145), channel_id=1, source_target_pairs={{0,2},{1,3},{2,0},{3,1},{4,6},{5,7},{6,4},{7,5},{8,10},{9,11},{10,... | collective-permute-start | bytes 786440 | tf_op jit(solution)/shard_map/ppermute | solution.py:21
  533.1 36.1 %collective-permute-start.94 = (bf16[128,1024]{1,0:T(8,128)(2,1)S(1)}, bf16[128,1024]{1,0:T(8,128)(2,1)S(1)}, u32[]{:S(2)}, u32[]{:S(2)}) collective-permute-start(bf16[128,1024]{1,0:T(8,128)(2,1)S(1)} %slice.1144), channel_id=1, source_target_pairs={{0,2},{1,3},{2,0},{3,1},{4,6},{5,7},{6,4},{7,5},{8,10},{9,11},{10,... | collective-permute-start | bytes 786440 | tf_op jit(solution)/shard_map/ppermute | solution.py:21
  (298 other events, 2702.8 us)

commit v2 on v1

v2 whole, which is shorter than its diff:
```python
import jax
import jax.numpy as jnp
from jax import lax
from jax.sharding import PartitionSpec as P

HEAD_DIM = 128
eps_norm = 1e-05
eps_batch = 1e-05
bf16 = jnp.bfloat16
f32 = jnp.float32


def mm(left, right, left_dim, right_dim):
    return lax.dot_general(
        left, right, (((left_dim,), (right_dim,)), ((), ())), preferred_element_type=f32
    )


def swap(value, axis, distance):
    pairs = [(index, index ^ distance) for index in range(lax.axis_size(axis))]
    return lax.ppermute(value, axis, pairs)


class Cube:
    def __init__(self, size):
        self.bits = size.bit_length() - 1
        middle = tuple(range(self.bits - 1, 0, -1))
        self.first = middle + (0,)
        self.second = middle[::-1] + (0,)
        self.order = sorted(range(size), key=self.key)

    def key(self, label):
        return sum(((label >> bit) & 1) << place for place, bit in enumerate(self.first))

    def runs(self, entries):
        joined = []
        for source, place in entries:
            if joined and joined[-1][0] == source and joined[-1][2] == place:
                joined[-1][2] = place + 1
            else:
                joined.append([source, place, place + 1])
        return joined

    def rows(self, sources, entries, height):
        parts = [
            lax.slice_in_dim(sources[source], low * height, high * height, axis=0)
            for source, low, high in self.runs(entries)
        ]
        return parts[0] if len(parts) == 1 else jnp.concatenate(parts, axis=0)

    def gather(self, shard, order):
        height = shard.shape[0]
        held, labels = shard, [0]
        for bit in order[:-1]:
            taken = yield held, "dp", 1 << bit
            entries = [(label, 0, place) for place, label in enumerate(labels)]
            entries += [(label ^ (1 << bit), 1, place) for place, label in enumerate(labels)]
            entries.sort(key=lambda entry: self.key(entry[0]))
            held = self.rows((held, taken), [entry[1:] for entry in entries], height)
            labels = [entry[0] for entry in entries]
        taken = yield held, "dp", 1
        return held, taken

    def scatter(self, low, high, order):
        labels = [label for label in self.order if not label & 1]
        height = low.shape[0] // len(labels)
        taken = yield high, "dp", 1
        held = low.astype(f32) + taken.astype(f32)
        for bit in order[-2::-1]:
            held = held.astype(bf16)
            send = [(0, place) for place, label in enumerate(labels) if label >> bit & 1]
            keep = [(0, place) for place, label in enumerate(labels) if not label >> bit & 1]
            taken = yield self.rows((held,), send, height), "dp", 1 << bit
            held = self.rows((held,), keep, height).astype(f32) + taken.astype(f32)
            labels = [label for label in labels if not label >> bit & 1]
        return held


class Move:
    def __init__(self, steps, left=1):
        self.steps, self.left, self.result = steps, left, None
        self.request = next(steps)

    def advance(self, taken):
        self.left -= 1
        try:
            self.request = self.steps.send(taken)
        except StopIteration as end:
            self.request, self.result = None, end.value


def once(value, axis, distance):
    taken = yield value, axis, distance
    return taken


def tie(*values):
    return lax.optimization_barrier(values)


def issue(anchor, *moves):
    *values, anchor = tie(*[move.request[0] for move in moves], anchor)
    for move, value in zip(moves, values):
        move.flying = swap(value, *move.request[1:])
    return anchor


def wait(anchor, *moves):
    *values, anchor = tie(*[move.flying for move in moves], anchor)
    for move, value in zip(moves, values):
        move.advance(value)
    return anchor


def fly(anchor, left, *moves):
    while moves[0].left > left:
        anchor = wait(issue(anchor, *moves), *moves)
    return issue(anchor, *moves)


def halves(value):
    middle = value.shape[-1] // 2
    return value[..., :middle], value[..., middle:]


def span_mask(starts, span_length, length):
    frames = jnp.arange(length, dtype=jnp.int32)
    finish = starts + span_length[:, None]
    inside = (frames[None, None, :] >= starts[:, :, None]) & (
        frames[None, None, :] < finish[:, :, None]
    )
    return jnp.any(inside, axis=1)


def normalize(stream, norm_gain):
    centred = stream - jnp.mean(stream, axis=-1, keepdims=True)
    inverse = lax.rsqrt(jnp.mean(centred * centred, axis=-1, keepdims=True) + eps_norm)
    scaled = centred * inverse
    return (scaled * norm_gain, scaled, inverse)


def normalize_back(grad_normed, scaled, inverse, norm_gain):
    grad_scaled = grad_normed * norm_gain
    grad_gain = jnp.sum(grad_normed * scaled, axis=0)
    centre_term = jnp.mean(grad_scaled, axis=-1, keepdims=True)
    slope_term = jnp.mean(grad_scaled * scaled, axis=-1, keepdims=True)
    return (inverse * (grad_scaled - centre_term - scaled * slope_term), grad_gain)


def swish_slope(values):
    logistic = jax.nn.sigmoid(values)
    return logistic + values * logistic * (1.0 - logistic)


def pair_sum(partial_value):
    mine = partial_value.astype(bf16)
    taken = yield mine, "tp", 1
    return mine.astype(f32) + taken.astype(f32)


def project_in(normed, weight):
    return sum(mm(part, rows, 1, 0) for part, rows in zip(halves(normed), weight))


def project_out(active, weight):
    return jnp.concatenate([mm(active, rows, 1, 1) for rows in weight], axis=1)


def outer(rows_side, columns_side):
    return [mm(part, columns_side, 0, 0).astype(bf16) for part in halves(rows_side)]


def ffn_forward(whole_in, weight_in, weight_out):
    hidden = project_in(whole_in, weight_in)
    active = (hidden * jax.nn.sigmoid(hidden)).astype(bf16)
    return project_out(active, weight_out), (hidden, active)


def ffn_backward(whole_grad, state, weight_in, weight_out):
    grad_active = project_in(whole_grad, weight_out)
    grad_hidden = (grad_active * swish_slope(state[0])).astype(bf16)
    return project_out(grad_hidden, weight_in), grad_hidden


def split_heads(project):
    quarter = project.shape[1] // 2
    width = quarter // 3
    pieces = []
    for kind in range(3):
        columns = [
            base + kind * width + head
            for base in (0, quarter)
            for head in range(0, width, HEAD_DIM)
        ]
        pieces.append(jnp.stack([project[:, at : at + HEAD_DIM] for at in columns]))
    return pieces


def merge_heads(pieces):
    heads = pieces[0].shape[0] // 2
    return jnp.concatenate(
        [
            piece[base + head]
            for base in (0, heads)
            for piece in pieces
            for head in range(heads)
        ],
        axis=1,
    )


def attn_forward(whole_in, weight_in):
    project = project_in(whole_in, weight_in).astype(bf16)
    queries, key_rows, value_rows = split_heads(project)
    scores = jnp.einsum(
        "hqe,hke->hqk", queries, key_rows, preferred_element_type=f32
    ) * HEAD_DIM ** (-0.5)
    highest = jnp.max(scores, axis=-1, keepdims=True)
    raised = jnp.exp(scores - highest)
    probs = raised / jnp.sum(raised, axis=-1, keepdims=True)
    mixed = jnp.einsum(
        "hqk,hke->hqe", probs.astype(bf16), value_rows, preferred_element_type=f32
    ).astype(bf16)
    mixed = jnp.concatenate([mixed[head] for head in range(mixed.shape[0])], axis=1)
    return mixed, (queries, key_rows, value_rows, probs)


def attn_backward(whole_grad, saved, weight_out):
    queries, key_rows, value_rows, probs = saved
    grad_mixed = project_in(whole_grad, weight_out).astype(bf16)
    heads = queries.shape[0]
    grad_mixed = jnp.stack(
        [grad_mixed[:, head * HEAD_DIM : (head + 1) * HEAD_DIM] for head in range(heads)]
    )
    factor = HEAD_DIM ** (-0.5)
    grad_values = jnp.einsum(
        "hqk,hqe->hke", probs.astype(bf16), grad_mixed, preferred_element_type=f32
    )
    grad_probs = jnp.einsum("hqe,hke->hqk", grad_mixed, value_rows, preferred_element_type=f32)
    grad_scores = (
        probs * (grad_probs - jnp.sum(probs * grad_probs, axis=-1, keepdims=True))
    ).astype(bf16)
    grad_queries = (
        jnp.einsum("hqk,hke->hqe", grad_scores, key_rows, preferred_element_type=f32) * factor
    )
    grad_keys = (
        jnp.einsum("hqk,hqe->hke", grad_scores, queries, preferred_element_type=f32) * factor
    )
    return merge_heads([part.astype(bf16) for part in (grad_queries, grad_keys, grad_values)])


def sum_items(rows):
    for bit in range(lax.axis_size("dp").bit_length() - 1):
        rows = rows + swap(rows, "dp", 1 << bit)
    other = swap(rows, "tp", 2)
    first, second = halves(other)
    return rows + jnp.concatenate([second, first], axis=-1)


def shifted(value, amount):
    frames = value.shape[0]
    if amount == 0:
        return value
    edge = jnp.zeros((abs(amount), value.shape[1]), value.dtype)
    if amount > 0:
        return jnp.concatenate([value[amount:], edge], axis=0)
    return jnp.concatenate([edge, value[: frames + amount]], axis=0)


def value_gate(paired):
    quarter = paired.shape[1] // 2
    width = quarter // 2
    return [
        jnp.concatenate(
            [paired[:, at : at + width] for at in (kind * width, quarter + kind * width)], axis=1
        )
        for kind in (0, 1)
    ]


def depth_mix(kernel_local, value, sign):
    reach = kernel_local.shape[0] // 2
    return sum(
        kernel_local[offset] * shifted(value, sign * (offset - reach))
        for offset in range(kernel_local.shape[0])
    )


def conv_backward(grad_batched, sums, saved, kernel_local, batch_gain, population):
    values_part, gate, gated, normal, batch_inverse = saved
    grad_bias, grad_scale = sums
    grad_depth = (
        batch_inverse
        * batch_gain
        * (grad_batched - grad_bias / population - normal * (grad_scale / population))
    )
    taps = kernel_local.shape[0]
    grad_kernel = jnp.stack(
        [jnp.sum(grad_depth * shifted(gated, tap - taps // 2), axis=0) for tap in range(taps)]
    )
    grad_gated = depth_mix(kernel_local, grad_depth, -1)
    logistic = jax.nn.sigmoid(gate)
    first, second = halves((grad_gated * logistic).astype(bf16))
    third, fourth = halves((grad_gated * values_part * logistic * (1.0 - logistic)).astype(bf16))
    return jnp.concatenate([first, third, second, fourth], axis=1), grad_kernel


def pick(value, index):
    return lax.dynamic_index_in_dim(value, index, 0, keepdims=False)


def on_device(
    feats,
    noise,
    starts,
    span_length,
    cotangent,
    norm_gains,
    ffn1_in,
    ffn1_out,
    qkv_weight,
    attn_out,
    conv_in,
    conv_kernel,
    batch_gain,
    batch_bias,
    conv_out,
    ffn2_in,
    ffn2_out,
):
    local_frames, width = feats.shape[1], feats.shape[2]
    parts = lax.axis_size("tp")
    replicas = lax.axis_size("dp")
    assert parts == 4 and feats.shape[0] == 2
    whole_frames = local_frames * parts
    population = whole_frames * feats.shape[0] * replicas
    place = lax.axis_index("tp")
    item = place // 2
    channels = batch_gain.shape[0]
    cube = Cube(replicas)
    block = width // replicas

    columns = jnp.arange(width, dtype=jnp.int32)
    position = sum(
        jnp.where(columns // block == at, label, 0) for at, label in enumerate(cube.order)
    )
    source = (position ^ lax.axis_index("dp")) * block + columns % block
    moved = columns[:, None] == source[None, :]

    def to_stream(rows):
        return mm(rows, moved.astype(rows.dtype), 1, 0)

    def exact(rows, contract):
        return lax.dot_general(
            rows,
            moved.astype(f32),
            (((1,), (contract,)), ((), ())),
            precision=lax.Precision.HIGHEST,
        )

    steps = cube.bits

    def gathering(shard, order):
        return Move(cube.gather(shard, order), steps)

    def scattering(low_high, order):
        return Move(cube.scatter(*low_high, order), steps)

    def across(value):
        return Move(once(value, "tp", 2))

    masked = span_mask(starts, span_length, whole_frames)
    local_mask = lax.dynamic_slice_in_dim(masked, place * local_frames, local_frames, 1)[:, :, None]
    entered = jnp.where(local_mask, noise, feats)
    pulled = jnp.where(local_mask, cotangent, jnp.zeros((), bf16))
    rows, hidden_width = ffn1_in.shape

    def whole_item(own, other):
        relative = jnp.stack([own[0], other[0], own[1], other[1]])
        ordered = jnp.stack([pick(relative, place ^ chunk) for chunk in range(parts)])
        return to_stream(ordered.reshape(whole_frames, width))

    anchor = span_length
    first_own = gathering(ffn1_in, cube.first), gathering(ffn1_out, cube.second)
    first_swap = across(ffn1_in), across(ffn1_out)
    item_swap = across(pick(entered, 1 - item))
    anchor = issue(anchor, *first_own, first_swap[0], item_swap)
    anchor = wait(anchor, *first_own, first_swap[0], item_swap)
    anchor = fly(anchor, 2, *first_own)
    anchor = issue(anchor, first_swap[1])
    anchor = wait(anchor, *first_own, first_swap[1])
    near = jnp.stack([pick(entered, item), item_swap.result])
    far = Move(once(near, "tp", 1))
    first_other = (
        gathering(first_swap[0].result, cube.first),
        gathering(first_swap[1].result, cube.second),
    )
    anchor = issue(anchor, *first_own, *first_other, far)
    anchor = wait(anchor, *first_own, *first_other, far)
    attn_shard = jnp.concatenate([qkv_weight.reshape(rows, -1), attn_out], axis=1)
    attn_swap = across(attn_shard)
    anchor = fly(anchor, 2, *first_other)
    anchor = issue(anchor, attn_swap)
    stream = whole_item(near, far.result)
    gains = exact(norm_gains, 0)
    normed, first_scaled, first_inverse = normalize(stream, gains[0])
    first_input = normed.astype(bf16)
    first_weights = [[move.result for move in first_own]]
    partial_own, state = ffn_forward(first_input, *first_weights[0])
    first_states = [state]
    anchor = wait(anchor, *first_other)
    anchor = wait(anchor, attn_swap)

    def doubled(shard, other):
        return jnp.concatenate([shard, other], axis=1)

    qkv_width = 3 * qkv_weight.shape[2]
    attn_moves = (
        gathering(
            doubled(attn_shard[:, :qkv_width], attn_swap.result[:, :qkv_width]), cube.first
        ),
        gathering(
            doubled(attn_shard[:, qkv_width:], attn_swap.result[:, qkv_width:]), cube.second
        ),
    )
    anchor = issue(anchor, *first_other, *attn_moves)
    anchor = wait(anchor, *first_other)
    conv_shard = jnp.concatenate([conv_in.reshape(rows, -1), conv_out], axis=1)
    conv_swap, pulled_swap = across(conv_shard), across(pick(pulled, 1 - item))
    anchor = issue(anchor, conv_swap, pulled_swap)
    first_weights.append([move.result for move in first_other])
    partial_value, state = ffn_forward(first_input, *first_weights[1])
    first_states.append(state)
    pair = Move(pair_sum(partial_own + partial_value))
    anchor = wait(anchor, *attn_moves)
    anchor = fly(anchor, 2, *attn_moves)
    anchor = issue(anchor, pair)
    anchor = wait(anchor, pair)
    stream = stream + 0.5 * pair.result

    normed, attn_scaled, attn_inverse = normalize(stream, gains[1])
    attn_input = normed.astype(bf16)
    anchor = wait(anchor, *attn_moves, conv_swap, pulled_swap)
    conv_width = 2 * conv_in.shape[2]
    conv_moves = (
        gathering(
            doubled(conv_shard[:, :conv_width], conv_swap.result[:, :conv_width]), cube.second
        ),
        gathering(
            doubled(conv_shard[:, conv_width:], conv_swap.result[:, conv_width:]), cube.first
        ),
    )
    pulled_near = jnp.stack([pick(pulled, item), pulled_swap.result])
    pulled_far = Move(once(pulled_near, "tp", 1))
    second_swap = across(ffn2_in), across(ffn2_out)
    anchor = issue(anchor, *attn_moves, *conv_moves, pulled_far, *second_swap)
    anchor = wait(anchor, *attn_moves)
    attn_weights = [move.result for move in attn_moves]
    mixed, attn_saved = attn_forward(attn_input, attn_weights[0])
    pair = Move(pair_sum(project_out(mixed, attn_weights[1])))
    anchor = wait(anchor, *conv_moves, pulled_far)
    anchor = fly(anchor, 2, *conv_moves)
    anchor = issue(anchor, pair)
    anchor = wait(anchor, pair)
    stream = stream + pair.result
    seed = whole_item(pulled_near, pulled_far.result)

    normed, conv_scaled, conv_inverse = normalize(stream, gains[2])
    conv_input = normed.astype(bf16)
    anchor = wait(anchor, *conv_moves)
    batch_pair = jnp.stack([batch_gain, batch_bias])
    batch_other = across(batch_pair)
    second_own = gathering(ffn2_in, cube.first), gathering(ffn2_out, cube.second)
    anchor = issue(anchor, *conv_moves, batch_other, *second_own)
    anchor = wait(anchor, *conv_moves, batch_other)
    batch_gain, batch_bias = jnp.concatenate([batch_pair, batch_other.result], axis=1)
    kernel_local = jnp.concatenate(
        [
            lax.dynamic_slice_in_dim(conv_kernel, start * channels, channels, 1)
            for start in (place, place ^ 2)
        ],
        axis=1,
    )
    conv_weights = [move.result for move in conv_moves]
    values_part, gate = value_gate(project_in(conv_input, conv_weights[0]))
    gated = values_part * jax.nn.sigmoid(gate)
    depthwise = depth_mix(kernel_local, gated, 1)
    masked_own = jnp.sum(pick(masked, item).astype(f32))
    sums = sum_items(
        jnp.stack(
            [
                jnp.sum(depthwise, axis=0),
                jnp.sum(depthwise * depthwise, axis=0),
                jnp.broadcast_to(masked_own, depthwise.shape[1:]),
            ]
        )
    )
    anchor = wait(anchor, *second_own, *second_swap)
    anchor = fly(anchor, 2, *second_own)
    masked_total = sums[2, 0]
    average = sums[0] / population
    variance = sums[1] / population - average * average
    batch_inverse = lax.rsqrt(variance + eps_batch)
    normal = (depthwise - average) * batch_inverse
    batched = normal * batch_gain + batch_bias
    conv_active = (batched * jax.nn.sigmoid(batched)).astype(bf16)
    conv_saved = values_part, gate, gated, normal, batch_inverse
    pair = Move(pair_sum(project_out(conv_active, conv_weights[1])))
    anchor = wait(anchor, *second_own)
    second_other = (
        gathering(second_swap[0].result, cube.first),
        gathering(second_swap[1].result, cube.second),
    )
    anchor = issue(anchor, pair, *second_own, *second_other)
    anchor = wait(anchor, pair)
    stream = stream + pair.result

    normed, second_scaled, second_inverse = normalize(stream, gains[3])
    second_input = normed.astype(bf16)
    anchor = wait(anchor, *second_other, *second_own)
    anchor = fly(anchor, 2, *second_other)
    second_weights = [[move.result for move in second_own]]
    partial_own, state = ffn_forward(second_input, *second_weights[0])
    second_states = [state]
    anchor = wait(anchor, *second_other)
    anchor = issue(anchor, *second_other)
    anchor = wait(anchor, *second_other)
    second_weights.append([move.result for move in second_other])
    partial_value, state = ffn_forward(second_input, *second_weights[1])
    second_states.append(state)
    pair = Move(pair_sum(partial_own + partial_value))
    anchor = issue(anchor, pair)
    anchor = wait(anchor, pair)
    stream = stream + 0.5 * pair.result
    final_out, final_scaled, final_inverse = normalize(stream, gains[4])

    def leaving(value):
        chunks = value.astype(bf16).reshape(parts, local_frames, width)
        both = jnp.concatenate([pick(chunks, place), pick(chunks, place ^ 2)], axis=0)
        both = mm(both, moved.astype(bf16), 1, 1)
        return both[:local_frames], across(both[local_frames:].astype(bf16))

    def landed(mine, move):
        other = move.result.astype(f32)
        return jnp.stack([jnp.where(item == 0, mine, other), jnp.where(item == 0, other, mine)])

    out_mine, out_move = leaving(final_out)
    grad_stream, gain_final = normalize_back(
        seed * jnp.sqrt(population / masked_total), final_scaled, final_inverse, gains[4]
    )
    whole_grad = (0.5 * grad_stream).astype(bf16)
    partial_value, second_hidden = 0.0, []
    for state, weights in zip(second_states, second_weights):
        part, grad_hidden = ffn_backward(whole_grad, state, *weights)
        partial_value = partial_value + part
        second_hidden.append(grad_hidden)
    pair = Move(pair_sum(partial_value))
    anchor = issue(anchor, pair)
    second_out = [
        (
            scattering(outer(second_input, second_hidden[quarter]), cube.first),
            scattering(outer(whole_grad, second_states[quarter][1]), cube.second),
        )
        for quarter in (0, 1)
    ]
    anchor = wait(anchor, pair)
    anchor = issue(anchor, *second_out[1], out_move)
    grad_local, gain_second = normalize_back(
        pair.result, second_scaled, second_inverse, gains[3]
    )
    grad_stream = grad_stream + grad_local

    whole_grad = grad_stream.astype(bf16)
    grad_batched = project_in(whole_grad, conv_weights[1]) * swish_slope(batched)
    grad_bias, grad_scale = sums = sum_items(
        jnp.stack([jnp.sum(grad_batched, axis=0), jnp.sum(grad_batched * normal, axis=0)])
    )
    anchor = wait(anchor, *second_out[1], out_move)
    anchor = issue(anchor, *second_out[1])
    grad_paired, kernel_part = conv_backward(
        grad_batched, sums, conv_saved, kernel_local, batch_gain, population
    )
    pair = Move(pair_sum(project_out(grad_paired, conv_weights[0])))
    anchor = wait(anchor, *second_out[1])
    anchor = fly(anchor, 1, *second_out[1])
    anchor = issue(anchor, pair, *second_out[0])
    conv_out_moves = (
        scattering(outer(conv_input, grad_paired), cube.second),
        scattering(outer(whole_grad, conv_active), cube.first),
    )
    anchor = wait(anchor, pair)
    grad_local, gain_conv = normalize_back(pair.result, conv_scaled, conv_inverse, gains[2])
    grad_stream = grad_stream + grad_local

    whole_grad = grad_stream.astype(bf16)
    anchor = wait(anchor, *second_out[1], *second_out[0])

    def crossing(moves):
        return across(jnp.concatenate([move.result.astype(bf16) for move in moves], axis=1))

    def crossing_half(moves):
        return across(
            jnp.concatenate([halves(move.result)[1].astype(bf16) for move in moves], axis=1)
        )

    second_back = crossing(second_out[1])
    anchor = issue(anchor, *second_out[0], second_back)
    grad_project = attn_backward(whole_grad, attn_saved, attn_weights[1])
    pair = Move(pair_sum(project_out(grad_project, attn_weights[0])))
    anchor = wait(anchor, *second_out[0])
    anchor = fly(anchor, 1, *second_out[0])
    anchor = issue(anchor, pair, *conv_out_moves)
    attn_out_moves = (
        scattering(outer(attn_input, grad_project), cube.first),
        scattering(outer(whole_grad, mixed), cube.second),
    )
    anchor = wait(anchor, pair)
    grad_local, gain_attn = normalize_back(pair.result, attn_scaled, attn_inverse, gains[1])
    grad_stream = grad_stream + grad_local

    whole_grad = (0.5 * grad_stream).astype(bf16)
    anchor = wait(anchor, *second_out[0], *conv_out_moves, second_back)
    anchor = issue(anchor, *conv_out_moves, *attn_out_moves)
    first_out = [None, None]
    partial_value = 0.0
    for quarter in (1, 0):
        part, grad_hidden = ffn_backward(
            whole_grad, first_states[quarter], *first_weights[quarter]
        )
        partial_value = partial_value + part
        first_out[quarter] = (
            scattering(outer(first_input, grad_hidden), cube.first),
            scattering(outer(whole_grad, first_states[quarter][1]), cube.second),
        )
    pair = Move(pair_sum(partial_value))
    anchor = wait(anchor, *conv_out_moves, *attn_out_moves)
    anchor = fly(anchor, 1, *conv_out_moves)
    anchor = issue(anchor, *first_out[1])
    anchor = wait(anchor, *first_out[1])
    anchor = issue(anchor, pair, *first_out[1])
    anchor = wait(anchor, *conv_out_moves)
    conv_back = crossing_half(conv_out_moves)
    anchor = wait(anchor, pair)
    grad_local, gain_first = normalize_back(pair.result, first_scaled, first_inverse, gains[0])
    grad_stream = grad_stream + grad_local
    mask_own = pick(masked, item)[:, None]
    feats_mine, feats_move = leaving(jnp.where(mask_own, 0.0, grad_stream))
    anchor = wait(anchor, *first_out[1])
    anchor = fly(anchor, 1, *first_out[1])
    anchor = issue(anchor, *first_out[0], feats_move)
    anchor = wait(anchor, *first_out[1], *first_out[0], feats_move)
    first_back = crossing(first_out[1])
    anchor = issue(anchor, first_back, *attn_out_moves)

    gain_grads = jnp.stack((gain_first, gain_attn, gain_conv, gain_second, gain_final))
    gain_grads = 0.5 * exact(gain_grads, 1)
    kernel_full = jnp.zeros(conv_kernel.shape, f32)
    for quarter, start in enumerate((place, place ^ 2)):
        kernel_full = lax.dynamic_update_slice_in_dim(
            kernel_full,
            kernel_part[:, quarter * channels : (quarter + 1) * channels],
            start * channels,
            1,
        )
    small = jnp.concatenate([gain_grads, kernel_full], axis=0)
    for bit in range(steps):
        small = small + swap(small, "dp", 1 << bit)
    small = small + swap(small, "tp", 2)
    small = small + swap(small, "tp", 1)
    norms = norm_gains.shape[0]

    anchor = wait(anchor, *attn_out_moves)
    anchor = fly(anchor, 1, *attn_out_moves)
    anchor = issue(anchor, conv_back)
    anchor = wait(anchor, *attn_out_moves)
    attn_back = crossing_half(attn_out_moves)
    anchor = issue(anchor, *first_out[0], attn_back)
    anchor = wait(anchor, *first_out[0])
    anchor = fly(anchor, 1, *first_out[0])
    anchor = wait(anchor, *first_out[0], first_back, conv_back, attn_back)

    def kept(moves, back, split):
        first, second = [halves(move.result)[0] if split else move.result for move in moves]
        other = back.result.astype(f32)
        return first + other[:, : first.shape[1]], second + other[:, first.shape[1] :]

    first_in_grad, first_out_grad = kept(first_out[0], first_back, False)
    second_in_grad, second_out_grad = kept(second_out[0], second_back, False)
    qkv_grad, attn_out_grad = kept(attn_out_moves, attn_back, True)
    conv_in_grad, conv_out_grad = kept(conv_out_moves, conv_back, True)
    return (
        landed(out_mine, out_move),
        landed(feats_mine, feats_move),
        masked_total,
        small[:norms],
        first_in_grad,
        first_out_grad,
        qkv_grad.reshape(qkv_weight.shape),
        attn_out_grad,
        conv_in_grad.reshape(conv_in.shape),
        small[norms:],
        grad_scale[:channels],
        grad_bias[:channels],
        conv_out_grad,
        second_in_grad,
        second_out_grad,
    )


def solution(mesh):
    return jax.shard_map(
        on_device,
        mesh=mesh,
        in_specs=(
            P("dp", "tp", None),
            P("dp", "tp", None),
            P("dp", None),
            P("dp"),
            P("dp", "tp", None),
            P(),
            P("dp", "tp"),
            P("dp", "tp"),
            P("dp", None, "tp"),
            P("dp", "tp"),
            P("dp", None, "tp"),
            P(),
            P("tp"),
            P("tp"),
            P("dp", "tp"),
            P("dp", "tp"),
            P("dp", "tp"),
        ),
        out_specs=(
            P("dp", "tp", None),
            P("dp", "tp", None),
            P(),
            P(),
            P("dp", "tp"),
            P("dp", "tp"),
            P("dp", None, "tp"),
            P("dp", "tp"),
            P("dp", None, "tp"),
            P(),
            P("tp"),
            P("tp"),
            P("dp", "tp"),
            P("dp", "tp"),
            P("dp", "tp"),
        ),
        check_vma=False,
    )
```

time: 585 us -> 570 us (0.974)
  waiting for transfers between devices: 302 us -> 257 us
  matrix products: 76.4 us -> 88.5 us
  starting transfers between devices: 88.9 us -> 99.2 us
  other arithmetic: 55.3 us -> 62.7 us
    ppermute x95 -> x110, waiting for transfers between devices: 302 us -> 257 us  [swap(): return lax.ppermute(value, axis, pairs)]
    dot_general x63 -> x76, matrix products: 66.8 us -> 80.2 us  [mm(): lax.dot_general(left, right, (((left_dim,), (right_dim,)), ((), ())), pre...]
    ppermute x95 -> x110, starting transfers between devices: 88.9 us -> 99.2 us  [swap(): return lax.ppermute(value, axis, pairs)]
    convert_element_type x10 -> x24, other arithmetic: 3.11 us -> 13 us  [scatter(): held = held.astype(bf16)]
    unnamed x479 -> x519, local copies, waits for them, and re-layouts: 29.7 us -> 29.4 us
  transfers between devices with their start and end apart: 95 -> 110, of which waited for: 43 -> 50; matrix products, arithmetic and copies ran while one was open for 23% -> 20% of each run, Pallas kernels for 0% -> 0%
where the time goes in v2:
time: 570 us; the launch traced here: 559 us
  waiting for transfers between devices  257 us (45%)
  starting transfers between devices  99.2 us (17%)
  matrix products  88.5 us (16%)
  other arithmetic  62.7 us (11%)
  local copies, waits for them, and re-layouts  44.8 us (8%)
  between operations  6.15 us (1%)
    ppermute x110, waiting for transfers between devices, swap(): return lax.ppermute(value, axis, pairs)  257 us
    ppermute x110, starting transfers between devices, swap(): return lax.ppermute(value, axis, pairs)  99.2 us
    dot_general x76, matrix products, mm(): lax.dot_general(left, right, (((left_dim,), (right_dim,)), ((), ())), pre...  80.2 us
    unnamed x519, local copies, waits for them, and re-layouts  29.4 us
    convert_element_type x24, other arithmetic, scatter(): held = held.astype(bf16)  13 us
  transfers between devices with their start and end apart: 110, of which 50 were waited for; matrix products, arithmetic and copies ran while one was open for 20% of the time, Pallas kernels for 0%

profile of v2, /device:TPU:0, one launch (start us, length us, event | category | flops | bytes accessed | tf_op | source)
XLA Modules:
  0.0 558.9 jit_solution(12480869556293043459)
XLA Ops:
  11.7 16.7 %collective-permute-done.3 = bf16[64,1024]{1,0:T(8,128)(2,1)S(1)} collective-permute-done((bf16[64,1024]{1,0:T(8,128)(2,1)S(1)}, bf16[64,1024]{1,0:T(8,128)(2,1)S(1)}, u32[]{:S(2)}, u32[]{:S(2)}) %collective-permute-start.3) | collective-permute-done | bytes 131104 | tf_op jit(solution)/shard_map/ppermute | solution.py:21
  31.7 11.0 %collective-permute-done.6 = bf16[128,1024]{1,0:T(8,128)(2,1)} collective-permute-done((bf16[128,1024]{1,0:T(8,128)(2,1)S(1)}, bf16[128,1024]{1,0:T(8,128)(2,1)}, u32[]{:S(2)}, u32[]{:S(2)}) %collective-permute-start.6) | collective-permute-done | bytes 262176 | tf_op jit(solution)/shard_map/ppermute | solution.py:21
  66.9 7.9 %collective-permute-done.12 = bf16[256,1024]{1,0:T(8,128)(2,1)S(1)} collective-permute-done((bf16[256,1024]{1,0:T(8,128)(2,1)S(1)}, bf16[256,1024]{1,0:T(8,128)(2,1)S(1)}, u32[]{:S(2)}, u32[]{:S(2)}) %collective-permute-start.12) | collective-permute-done | bytes 524320 | tf_op jit(solution)/shard_map/ppermute | solution.py:21
  90.6 5.0 collective-permute-done.17
  102.5 15.4 %collective-permute-done.19 = bf16[256,1024]{1,0:T(8,128)(2,1)S(1)} collective-permute-done((bf16[256,1024]{1,0:T(8,128)(2,1)S(1)}, bf16[256,1024]{1,0:T(8,128)(2,1)S(1)}, u32[]{:S(2)}, u32[]{:S(2)}) %collective-permute-start.19) | collective-permute-done | bytes 524320 | tf_op jit(solution)/shard_map/ppermute | solution.py:21
  151.8 12.2 %collective-permute-done.29 = bf16[256,1024]{1,0:T(8,128)(2,1)S(1)} collective-permute-done((bf16[256,1024]{1,0:T(8,128)(2,1)S(1)}, bf16[256,1024]{1,0:T(8,128)(2,1)S(1)}, u32[]{:S(2)}, u32[]{:S(2)}) %collective-permute-start.29) | collective-permute-done | bytes 524320 | tf_op jit(solution)/shard_map/ppermute | solution.py:21
  166.1 7.2 %collective-permute-done.34 = f32[2,256]{1,0:T(2,128)S(1)} collective-permute-done((f32[2,256]{1,0:T(2,128)S(1)}, f32[2,256]{1,0:T(2,128)S(1)}, u32[]{:S(2)}, u32[]{:S(2)}) %collective-permute-start.34) | collective-permute-done | bytes 2080 | tf_op jit(solution)/shard_map/ppermute | solution.py:21
  188.0 9.8 %collective-permute-done.37 = f32[3,512]{1,0:T(4,128)S(1)} collective-permute-done((f32[3,512]{1,0:T(4,128)S(1)}, f32[3,512]{1,0:T(4,128)S(1)}, u32[]{:S(2)}, u32[]{:S(2)}) %collective-permute-start.37) | collective-permute-done | bytes 6176 | tf_op jit(solution)/shard_map/ppermute | solution.py:21
  210.8 7.2 %collective-permute-done.45 = bf16[256,1024]{1,0:T(8,128)(2,1)} collective-permute-done((bf16[256,1024]{1,0:T(8,128)(2,1)S(1)}, bf16[256,1024]{1,0:T(8,128)(2,1)}, u32[]{:S(2)}, u32[]{:S(2)}) %collective-permute-start.45) | collective-permute-done | bytes 524320 | tf_op jit(solution)/shard_map/ppermute | solution.py:21
  224.8 7.8 %collective-permute-done.50 = bf16[256,1024]{1,0:T(8,128)(2,1)S(1)} collective-permute-done((bf16[256,1024]{1,0:T(8,128)(2,1)S(1)}, bf16[256,1024]{1,0:T(8,128)(2,1)S(1)}, u32[]{:S(2)}, u32[]{:S(2)}) %collective-permute-start.50) | collective-permute-done | bytes 524320 | tf_op jit(solution)/shard_map/ppermute | solution.py:21
  252.5 9.5 %collective-permute-done.54 = bf16[256,1024]{1,0:T(8,128)(2,1)} collective-permute-done((bf16[256,1024]{1,0:T(8,128)(2,1)}, bf16[256,1024]{1,0:T(8,128)(2,1)}, u32[]{:S(2)}, u32[]{:S(2)}) %collective-permute-start.54) | collective-permute-done | bytes 524320 | tf_op jit(solution)/shard_map/ppermute | solution.py:21
  292.0 8.6 %collective-permute-done.55 = bf16[256,1024]{1,0:T(8,128)(2,1)S(1)} collective-permute-done((bf16[256,1024]{1,0:T(8,128)(2,1)S(1)}, bf16[256,1024]{1,0:T(8,128)(2,1)S(1)}, u32[]{:S(2)}, u32[]{:S(2)}) %collective-permute-start.55) | collective-permute-done | bytes 524320 | tf_op jit(solution)/shard_map/ppermute | solution.py:21
  329.6 9.8 %collective-permute-done.65 = bf16[256,1024]{1,0:T(8,128)(2,1)} collective-permute-done((bf16[256,1024]{1,0:T(8,128)(2,1)}, bf16[256,1024]{1,0:T(8,128)(2,1)}, u32[]{:S(2)}, u32[]{:S(2)}) %collective-permute-start.65) | collective-permute-done | bytes 524320 | tf_op jit(solution)/shard_map/ppermute | solution.py:21
  364.2 6.1 %collective-permute-done.72 = bf16[256,1024]{1,0:T(8,128)(2,1)S(1)} collective-permute-done((bf16[256,1024]{1,0:T(8,128)(2,1)S(1)}, bf16[256,1024]{1,0:T(8,128)(2,1)S(1)}, u32[]{:S(2)}, u32[]{:S(2)}) %collective-permute-start.72) | collective-permute-done | bytes 524320 | tf_op jit(solution)/shard_map/ppermute | solution.py:21
  408.3 7.8 %collective-permute-done.70 = bf16[256,1024]{1,0:T(8,128)(2,1)S(1)} collective-permute-done((bf16[256,1024]{1,0:T(8,128)(2,1)S(1)}, bf16[256,1024]{1,0:T(8,128)(2,1)S(1)}, u32[]{:S(2)}, u32[]{:S(2)}) %collective-permute-start.70) | collective-permute-done | bytes 524320 | tf_op jit(solution)/shard_map/ppermute | solution.py:21
  423.4 6.0 %collective-permute-done.77 = bf16[128,2048]{1,0:T(8,128)(2,1)S(1)} collective-permute-done((bf16[128,2048]{1,0:T(8,128)(2,1)S(1)}, bf16[128,2048]{1,0:T(8,128)(2,1)S(1)}, u32[]{:S(2)}, u32[]{:S(2)}) %collective-permute-start.77) | collective-permute-done | bytes 524320 | tf_op jit(solution)/shard_map/ppermute | solution.py:21
  434.4 6.3 %collective-permute-done.84 = bf16[256,1024]{1,0:T(8,128)(2,1)} collective-permute-done((bf16[256,1024]{1,0:T(8,128)(2,1)S(1)}, bf16[256,1024]{1,0:T(8,128)(2,1)}, u32[]{:S(2)}, u32[]{:S(2)}) %collective-permute-start.84) | collective-permute-done | bytes 524320 | tf_op jit(solution)/shard_map/ppermute | solution.py:21
  457.7 8.0 %collective-permute-done.95 = f32[10,1024]{1,0:T(8,128)S(1)} collective-permute-done((f32[10,1024]{1,0:T(8,128)S(1)}, f32[10,1024]{1,0:T(8,128)S(1)}, u32[]{:S(2)}, u32[]{:S(2)}) %collective-permute-start.95) | collective-permute-done | bytes 40992 | tf_op jit(solution)/shard_map/ppermute | solution.py:21
  478.4 7.4 %collective-permute-done.79 = bf16[256,512]{1,0:T(8,128)(2,1)S(1)} collective-permute-done((bf16[256,512]{1,0:T(8,128)(2,1)S(1)}, bf16[256,512]{1,0:T(8,128)(2,1)S(1)}, u32[]{:S(2)}, u32[]{:S(2)}) %collective-permute-start.79) | collective-permute-done | bytes 262176 | tf_op jit(solution)/shard_map/ppermute | solution.py:21
  497.4 9.7 %collective-permute-done.97 = bf16[256,1536]{1,0:T(8,128)(2,1)S(1)} collective-permute-done((bf16[256,1536]{1,0:T(8,128)(2,1)S(1)}, bf16[256,1536]{1,0:T(8,128)(2,1)S(1)}, u32[]{:S(2)}, u32[]{:S(2)}) %collective-permute-start.97) | collective-permute-done | bytes 786464 | tf_op jit(solution)/shard_map/ppermute | solution.py:21
  513.1 5.6 %collective-permute-done.107 = bf16[128,512]{1,0:T(8,128)(2,1)S(1)} collective-permute-done((bf16[128,512]{1,0:T(8,128)(2,1)S(1)}, bf16[128,512]{1,0:T(8,128)(2,1)S(1)}, u32[]{:S(2)}, u32[]{:S(2)}) %collective-permute-start.107) | collective-permute-done | bytes 131104 | tf_op jit(solution)/shard_map/ppermute | solution.py:21
  524.3 5.2 collective-permute-done.101
  535.1 13.6 %collective-permute-done.108 = bf16[128,768]{1,0:T(8,128)(2,1)S(1)} collective-permute-done((bf16[128,768]{1,0:T(8,128)(2,1)S(1)}, bf16[128,768]{1,0:T(8,128)(2,1)S(1)}, u32[]{:S(2)}, u32[]{:S(2)}) %collective-permute-start.108) | collective-permute-done | bytes 196640 | tf_op jit(solution)/shard_map/ppermute | solution.py:21
  548.7 5.2 collective-permute-done.109
  (1049 shorter events, 343.6 us)
Async XLA Ops:
  4.2 24.2 %collective-permute-start = (bf16[128,1024]{1,0:T(8,128)(2,1)S(1)}, bf16[128,1024]{1,0:T(8,128)(2,1)S(1)}, u32[]{:S(2)}, u32[]{:S(2)}) collective-permute-start(bf16[128,1024]{1,0:T(8,128)(2,1)S(1)} %copy-done.120), channel_id=1, source_target_pairs={{0,16},{4,20},{8,24},{12,28},{16,0},{20,4},{24,8},{28,12},{1,17},{... | collective-permute-start | bytes 786440 | tf_op jit(solution)/shard_map/ppermute | solution.py:21
  7.2 21.1 %collective-permute-start.1 = (bf16[128,1024]{1,0:T(8,128)(2,1)S(1)}, bf16[128,1024]{1,0:T(8,128)(2,1)S(1)}, u32[]{:S(2)}, u32[]{:S(2)}) collective-permute-start(bf16[128,1024]{1,0:T(8,128)(2,1)S(1)} %copy-done.129), channel_id=1, source_target_pairs={{0,8},{4,12},{8,0},{12,4},{16,24},{20,28},{24,16},{28,20},{1,9},{5... | collective-permute-start | bytes 786440 | tf_op jit(solution)/shard_map/ppermute | solution.py:21
  95.8 22.9 %collective-permute-start.20 = (bf16[256,1536]{0,1:T(8,128)(2,1)S(1)}, bf16[256,1536]{0,1:T(8,128)(2,1)S(1)}, u32[]{:S(2)}, u32[]{:S(2)}) collective-permute-start(bf16[256,1536]{0,1:T(8,128)(2,1)S(1)} %pad_maximum_fusion.6), channel_id=1, source_target_pairs={{0,8},{4,12},{8,0},{12,4},{16,24},{20,28},{24,16},{28,20},{1,9},{5... | collective-permute-start | bytes 2359304 | tf_op jit(solution)/shard_map/ppermute | solution.py:21
  148.9 28.5 %collective-permute-start.41 = (bf16[128,1024]{1,0:T(8,128)(2,1)S(1)}, bf16[128,1024]{1,0:T(8,128)(2,1)}, u32[]{:S(2)}, u32[]{:S(2)}) collective-permute-start(bf16[128,1024]{1,0:T(8,128)(2,1)S(1)} %copy-done.109), channel_id=1, source_target_pairs={{0,2},{1,3},{2,0},{3,1},{4,6},{5,7},{6,4},{7,5},{8,10},{9,11},{10,... | collective-permute-start | bytes 786440 | tf_op jit(solution)/shard_map/ppermute | solution.py:21
  151.4 26.0 %collective-permute-start.42 = (bf16[128,1024]{1,0:T(8,128)(2,1)S(1)}, bf16[128,1024]{1,0:T(8,128)(2,1)}, u32[]{:S(2)}, u32[]{:S(2)}) collective-permute-start(bf16[128,1024]{1,0:T(8,128)(2,1)S(1)} %copy-done.121), channel_id=1, source_target_pairs={{0,2},{1,3},{2,0},{3,1},{4,6},{5,7},{6,4},{7,5},{8,10},{9,11},{10,... | collective-permute-start | bytes 786440 | tf_op jit(solution)/shard_map/ppermute | solution.py:21
  317.1 39.3 %collective-permute-start.56 = (bf16[512,1024]{1,0:T(8,128)(2,1)}, bf16[512,1024]{1,0:T(8,128)(2,1)}, u32[]{:S(2)}, u32[]{:S(2)}) collective-permute-start(bf16[512,1024]{1,0:T(8,128)(2,1)} %convolution_convert_fusion.19), channel_id=1, source_target_pairs={{0,4},{4,0},{8,12},{12,8},{16,20},{20,16},{24,28},{28,24},{1,5},{5... | collective-permute-start | bytes 3145736 | tf_op jit(solution)/shard_map/ppermute | solution.py:21
  317.1 40.9 %collective-permute-start.57 = (bf16[512,1024]{1,0:T(8,128)(2,1)}, bf16[512,1024]{1,0:T(8,128)(2,1)}, u32[]{:S(2)}, u32[]{:S(2)}) collective-permute-start(bf16[512,1024]{1,0:T(8,128)(2,1)} %convolution_convert_fusion.18), channel_id=1, source_target_pairs={{0,4},{4,0},{8,12},{12,8},{16,20},{20,16},{24,28},{28,24},{1,5},{5... | collective-permute-start | bytes 3145736 | tf_op jit(solution)/shard_map/ppermute | solution.py:21
  317.6 38.3 %collective-permute-start.58 = (bf16[64,1024]{1,0:T(8,128)(2,1)}, bf16[64,1024]{1,0:T(8,128)(2,1)}, u32[]{:S(2)}, u32[]{:S(2)}) collective-permute-start(bf16[64,1024]{1,0:T(8,128)(2,1)} %slice.1177), channel_id=1, source_target_pairs={{0,2},{1,3},{2,0},{3,1},{4,6},{5,7},{6,4},{7,5},{8,10},{9,11},{10,... | collective-permute-start | bytes 393224 | tf_op jit(solution)/shard_map/ppermute | solution.py:21
  324.8 70.3 %collective-permute-start.68 = (bf16[512,1024]{1,0:T(8,128)(2,1)}, bf16[512,1024]{1,0:T(8,128)(2,1)}, u32[]{:S(2)}, u32[]{:S(2)}) collective-permute-start(bf16[512,1024]{1,0:T(8,128)(2,1)} %convolution_convert_fusion.17), channel_id=1, source_target_pairs={{0,4},{4,0},{8,12},{12,8},{16,20},{20,16},{24,28},{28,24},{1,5},{5... | collective-permute-start | bytes 3145736 | tf_op jit(solution)/shard_map/ppermute | solution.py:21
  339.5 55.8 %collective-permute-start.69 = (bf16[512,1024]{1,0:T(8,128)(2,1)S(1)}, bf16[512,1024]{1,0:T(8,128)(2,1)S(1)}, u32[]{:S(2)}, u32[]{:S(2)}) collective-permute-start(bf16[512,1024]{1,0:T(8,128)(2,1)S(1)} %copy-done.97), channel_id=1, source_target_pairs={{0,4},{4,0},{8,12},{12,8},{16,20},{20,16},{24,28},{28,24},{1,5},{5... | collective-permute-start | bytes 3145736 | tf_op jit(solution)/shard_map/ppermute | solution.py:21
  355.9 66.7 %collective-permute-start.75 = (bf16[512,1024]{1,0:T(8,128)(2,1)S(1)}, bf16[512,1024]{1,0:T(8,128)(2,1)S(1)}, u32[]{:S(2)}, u32[]{:S(2)}) collective-permute-start(bf16[512,1024]{1,0:T(8,128)(2,1)S(1)} %convolution_convert_fusion.13), channel_id=1, source_target_pairs={{0,4},{4,0},{8,12},{12,8},{16,20},{20,16},{24,28},{28,24},{1,5},{5... | collective-permute-start | bytes 3145736 | tf_op jit(solution)/shard_map/ppermute | solution.py:21
  361.5 30.0 %collective-permute-start.63 = (bf16[256,1024]{1,0:T(8,128)(2,1)S(1)}, bf16[256,1024]{1,0:T(8,128)(2,1)S(1)}, u32[]{:S(2)}, u32[]{:S(2)}) collective-permute-start(bf16[256,1024]{1,0:T(8,128)(2,1)S(1)} %slice.855), channel_id=1, source_target_pairs={{0,8},{4,12},{8,0},{12,4},{16,24},{20,28},{24,16},{28,20},{1,9},{5... | collective-permute-start | bytes 1572872 | tf_op jit(solution)/shard_map/ppermute | solution.py:21
  370.3 21.2 %collective-permute-start.64 = (bf16[256,1024]{1,0:T(8,128)(2,1)S(1)}, bf16[256,1024]{1,0:T(8,128)(2,1)S(1)}, u32[]{:S(2)}, u32[]{:S(2)}) collective-permute-start(bf16[256,1024]{1,0:T(8,128)(2,1)S(1)} %pad_maximum_fusion.32), channel_id=1, source_target_pairs={{0,16},{4,20},{8,24},{12,28},{16,0},{20,4},{24,8},{28,12},{1,17},{... | collective-permute-start | bytes 1572872 | tf_op jit(solution)/shard_map/ppermute | solution.py:21
  395.1 25.9 %collective-permute-start.76 = (bf16[512,512]{1,0:T(8,128)(2,1)S(1)}, bf16[512,512]{1,0:T(8,128)(2,1)S(1)}, u32[]{:S(2)}, u32[]{:S(2)}) collective-permute-start(bf16[512,512]{1,0:T(8,128)(2,1)S(1)} %copy-done.138), channel_id=1, source_target_pairs={{0,4},{4,0},{8,12},{12,8},{16,20},{20,16},{24,28},{28,24},{1,5},{5... | collective-permute-start | bytes 1572872 | tf_op jit(solution)/shard_map/ppermute | solution.py:21
  404.2 25.2 %collective-permute-start.77 = (bf16[128,2048]{1,0:T(8,128)(2,1)S(1)}, bf16[128,2048]{1,0:T(8,128)(2,1)S(1)}, u32[]{:S(2)}, u32[]{:S(2)}) collective-permute-start(bf16[128,2048]{1,0:T(8,128)(2,1)S(1)} %pad_maximum_fusion.34), channel_id=1, source_target_pairs={{0,2},{1,3},{2,0},{3,1},{4,6},{5,7},{6,4},{7,5},{8,10},{9,11},{10,... | collective-permute-start | bytes 1572872 | tf_op jit(solution)/shard_map/ppermute | solution.py:21
  422.7 29.5 %collective-permute-start.85 = (bf16[256,1024]{1,0:T(8,128)(2,1)}, bf16[256,1024]{1,0:T(8,128)(2,1)}, u32[]{:S(2)}, u32[]{:S(2)}) collective-permute-start(bf16[256,1024]{1,0:T(8,128)(2,1)} %slice.891), channel_id=1, source_target_pairs={{0,8},{4,12},{8,0},{12,4},{16,24},{20,28},{24,16},{28,20},{1,9},{5... | collective-permute-start | bytes 1572872 | tf_op jit(solution)/shard_map/ppermute | solution.py:21
  429.5 23.9 %collective-permute-start.86 = (bf16[256,1024]{1,0:T(8,128)(2,1)}, bf16[256,1024]{1,0:T(8,128)(2,1)}, u32[]{:S(2)}, u32[]{:S(2)}) collective-permute-start(bf16[256,1024]{1,0:T(8,128)(2,1)} %pad_maximum_fusion.29), channel_id=1, source_target_pairs={{0,16},{4,20},{8,24},{12,28},{16,0},{20,4},{24,8},{28,12},{1,17},{... | collective-permute-start | bytes 1572872 | tf_op jit(solution)/shard_map/ppermute | solution.py:21
  448.7 28.4 %collective-permute-start.89 = (bf16[512,1024]{1,0:T(8,128)(2,1)S(1)}, bf16[512,1024]{1,0:T(8,128)(2,1)S(1)}, u32[]{:S(2)}, u32[]{:S(2)}) collective-permute-start(bf16[512,1024]{1,0:T(8,128)(2,1)S(1)} %copy-done.99), channel_id=1, source_target_pairs={{0,4},{4,0},{8,12},{12,8},{16,20},{20,16},{24,28},{28,24},{1,5},{5... | collective-permute-start | bytes 3145736 | tf_op jit(solution)/shard_map/ppermute | solution.py:21
  449.0 29.3 %collective-permute-start.90 = (bf16[512,1024]{1,0:T(8,128)(2,1)S(1)}, bf16[512,1024]{1,0:T(8,128)(2,1)S(1)}, u32[]{:S(2)}, u32[]{:S(2)}) collective-permute-start(bf16[512,1024]{1,0:T(8,128)(2,1)S(1)} %copy-done.98), channel_id=1, source_target_pairs={{0,4},{4,0},{8,12},{12,8},{16,20},{20,16},{24,28},{28,24},{1,5},{5... | collective-permute-start | bytes 3145736 | tf_op jit(solution)/shard_map/ppermute | solution.py:21
  453.4 35.1 %collective-permute-start.80 = (bf16[512,1536]{1,0:T(8,128)(2,1)S(1)}, bf16[512,1536]{1,0:T(8,128)(2,1)S(1)}, u32[]{:S(2)}, u32[]{:S(2)}) collective-permute-start(bf16[512,1536]{1,0:T(8,128)(2,1)S(1)} %copy-done.91), channel_id=1, source_target_pairs={{0,4},{4,0},{8,12},{12,8},{16,20},{20,16},{24,28},{28,24},{1,5},{5... | collective-permute-start | bytes 4718600 | tf_op jit(solution)/shard_map/ppermute | solution.py:21
  511.9 36.9 %collective-permute-start.105 = (bf16[128,2048]{1,0:T(8,128)(2,1)S(1)}, bf16[128,2048]{1,0:T(8,128)(2,1)S(1)}, u32[]{:S(2)}, u32[]{:S(2)}) collective-permute-start(bf16[128,2048]{1,0:T(8,128)(2,1)S(1)} %pad_maximum_fusion.36), channel_id=1, source_target_pairs={{0,2},{1,3},{2,0},{3,1},{4,6},{5,7},{6,4},{7,5},{8,10},{9,11},{10,... | collective-permute-start | bytes 1572872 | tf_op jit(solution)/shard_map/ppermute | solution.py:21
  521.3 27.4 %collective-permute-start.108 = (bf16[128,768]{1,0:T(8,128)(2,1)S(1)}, bf16[128,768]{1,0:T(8,128)(2,1)S(1)}, u32[]{:S(2)}, u32[]{:S(2)}) collective-permute-start(bf16[128,768]{1,0:T(8,128)(2,1)S(1)} %pad_maximum_fusion.52), channel_id=1, source_target_pairs={{0,2},{1,3},{2,0},{3,1},{4,6},{5,7},{6,4},{7,5},{8,10},{9,11},{10,... | collective-permute-start | bytes 589832 | tf_op jit(solution)/shard_map/ppermute | solution.py:21
  522.4 31.5 %collective-permute-start.109 = (bf16[128,1024]{1,0:T(8,128)(2,1)S(1)}, bf16[128,1024]{1,0:T(8,128)(2,1)S(1)}, u32[]{:S(2)}, u32[]{:S(2)}) collective-permute-start(bf16[128,1024]{1,0:T(8,128)(2,1)S(1)} %pad_maximum_fusion.50), channel_id=1, source_target_pairs={{0,2},{1,3},{2,0},{3,1},{4,6},{5,7},{6,4},{7,5},{8,10},{9,11},{10,... | collective-permute-start | bytes 786440 | tf_op jit(solution)/shard_map/ppermute | solution.py:21
  532.2 21.8 %collective-permute-start.103 = (bf16[128,1024]{1,0:T(8,128)(2,1)S(1)}, bf16[128,1024]{1,0:T(8,128)(2,1)S(1)}, u32[]{:S(2)}, u32[]{:S(2)}) collective-permute-start(bf16[128,1024]{1,0:T(8,128)(2,1)S(1)} %slice.941), channel_id=1, source_target_pairs={{0,16},{4,20},{8,24},{12,28},{16,0},{20,4},{24,8},{28,12},{1,17},{... | collective-permute-start | bytes 786440 | tf_op jit(solution)/shard_map/ppermute | solution.py:21
  (334 other events, 2478.2 us)
